TPU v7x, 32 devices: a whole 2x2x4 slice. The times are simulated.
32 devices in a mesh: walk: 8 (over z, x), vec: 4 (over y, core).
Axes of the slice: x: 2, y: 2, z: 4, core: 2. Of those that a mesh axis runs over, the one named last changes fastest.
Arguments:
- walkers: bfloat16 [16, 2432, 768], P('walk')
- chol: bfloat16 [4, 8, 384, 4096], P('vec', 'walk'), may hold values from -6 to 6
- owners: int32 [4, 2], P('vec'), may hold values from 0 to 7
- branch_src: int32 [16], P('walk'), may hold values from 0 to 15, as said below
Outputs:
- branched: bfloat16 [16, 2432, 768], P('walk')
- force_bias: float32 [16, 8, 2], P('walk', 'vec')
- exchange: float32 [16, 2], P('walk')
Inputs may be any that keep to these rules, and one draw needn't show every extreme that they name: `branch_src`: slot s takes its walker from the 2 walkers of block s // 2, or of the block before or after it (blocks taken cyclically).
All inputs are finite; a program needn't handle non-finite values.
Results may differ from a plain program's by a relative error of at most 0.0052.
Values may be sent and summed in bfloat16 or wider, within the bound.
A program may use at most 192 MiB of HBM per device.

v0:
```python
import functools

import jax
import jax.numpy as jnp
from jax import lax
from jax.experimental import pallas as pl
from jax.experimental.pallas import tpu as pltpu
from jax.sharding import PartitionSpec as P

MESH = pl.DeviceIdType.MESH
CHUNKS = 24
PARTS = 2
SKEW = 2
AHEAD = 3
QUEUE = (12, 14, 16, 18)
LEAF = ((3, 6, 9, 12), (6, 9, 12, 15), (12, 17), (17, 22))
HUB = ((16, 18, 20, 22), (19, 21, 23, 25), (24, 29), (29, 200))


def flip(index):
    return index + 1 - 2 * lax.rem(index, 2)


def walker_values(matrix, state):
    electrons = matrix.shape[0]
    orbitals = matrix.shape[1] // 2
    p = state[:orbitals, :]
    o = state[orbitals:, :]
    x = jnp.dot(matrix[:, :orbitals], p, preferred_element_type=jnp.float32)
    y = jnp.dot(matrix[:, orbitals:], p, preferred_element_type=jnp.float32)
    m_re = (x[:, :electrons] - y[:, electrons:]).astype(jnp.bfloat16)
    m_im = (x[:, electrons:] + y[:, :electrons]).astype(jnp.bfloat16)
    u = jnp.dot(m_re, o, preferred_element_type=jnp.float32)
    v = jnp.dot(m_im, o, preferred_element_type=jnp.float32)
    g_re = u[:, :electrons] - v[:, electrons:]
    g_im = u[:, electrons:] + v[:, :electrons]
    t_re, t_im = g_re.T, g_im.T
    eye = (lax.broadcasted_iota(jnp.int32, g_re.shape, 0)
           == lax.broadcasted_iota(jnp.int32, g_re.shape, 1))
    return [
        jnp.sum(jnp.where(eye, g_re, 0.0)),
        jnp.sum(jnp.where(eye, g_im, 0.0)),
        jnp.sum(g_re * t_re - g_im * t_im),
        2.0 * jnp.sum(g_re * t_im),
    ]


def step_kernel(
    n_walk, n_vec, flags, slots, chol, walkers, table, partner, branched,
    home, away, own, up, down, cand_0, cand_1, sel, matrix, state, result,
    bcast_send, home_sem, away_send, away_sem, relay_send,
    up_send, up_sem, down_send, down_sem,
    x_send, x_sem, z_send, z_sem, local_sem,
    y_send, y_sem, d_send, d_sem, r_send, r_sem,
    by_send, by_sem, bd_send, bd_sem, br_send, br_sem, self_sem,
    load_sem, t_send, t_sem,
):
    walk, vec = lax.axis_index("walk"), lax.axis_index("vec")
    rows = n_walk // 2
    row, col = walk // 2, lax.rem(walk, 2)
    low = lax.rem(vec, 2)
    hub = low == col
    cand = (cand_0, cand_1)
    chunks, depth = home.shape[0], home.shape[1]
    per_dev = walkers.shape[0]
    quarter = sel.shape[1]
    piece = quarter // PARTS
    pieces = [(w, t) for t in range(PARTS) for w in range(per_dev)]
    flip_walk, flip_vec = flip(walk), flip(vec)
    far_vec = lax.rem(vec + 2, n_vec)
    z_next = lax.rem(row + 1 - 2 * col + rows, rows)
    z_to = {"walk": z_next * 2 + col, "vec": vec}
    across = {"walk": flip_walk, "vec": vec}
    mate = {"walk": walk, "vec": flip_vec}
    over = {"walk": walk, "vec": far_vec}
    above = {"walk": walk + 2, "vec": vec}
    below = {"walk": walk - 2, "vec": vec}
    row_up, row_down = lax.rem(row + 1, rows), lax.rem(row + rows - 1, rows)

    place = col * n_vec + vec
    readers = [({"walk": walk, "vec": lax.rem(vec + j, n_vec)}, place) for j in range(1, n_vec)]
    readers += [({"walk": flip_walk, "vec": lax.rem(vec + j, n_vec)}, place) for j in range(n_vec)]
    readers += [({"walk": row_up * 2, "vec": lax.rem(vec + j, n_vec)}, place + 2 * n_vec) for j in range(n_vec)]
    readers += [({"walk": row_down * 2 + 1, "vec": lax.rem(vec + j, n_vec)}, place + 2 * n_vec) for j in range(n_vec)]

    bar = pltpu.get_barrier_semaphore()
    for target in (
        [t for t, _ in readers[:2 * n_vec - 1]]
        + [{"walk": r * 2 + c, "vec": lax.rem(vec + j, n_vec)}
           for r in (row_up, row_down) for c in range(2) for j in range(n_vec)]
    ):
        pl.semaphore_signal(bar, inc=1, device_id=target, device_id_type=MESH)
    pl.semaphore_wait(bar, 6 * n_vec - 1)

    def remote(src, dst, send, recv, target):
        return pltpu.make_async_remote_copy(
            src_ref=src, dst_ref=dst, send_sem=send, recv_sem=recv,
            device_id=target, device_id_type=MESH)

    def chol_rows(k):
        return chol.at[0, 0, pl.ds(pl.multiple_of(k * depth, depth), depth)]

    def own_to_home(k):
        return pltpu.make_async_copy(chol_rows(k), home.at[k], home_sem.at[k])

    def own_to_mate(k):
        return remote(chol_rows(k), home.at[k], bcast_send.at[k], home_sem.at[k], mate)

    def own_across(k):
        return remote(chol_rows(k), away.at[k], away_send.at[k], away_sem.at[k], across)

    def away_to_mate(k):
        return remote(away.at[k], away.at[k], relay_send.at[k], away_sem.at[k], mate)

    def send_up(k):
        return remote(up.at[k], up.at[k], up_send.at[k], up_sem.at[k], above)

    def send_down(k):
        return remote(down.at[k], down.at[k], down_send.at[k], down_sem.at[k], below)

    def part(index, t):
        return pl.ds(pl.multiple_of(index * quarter + t * piece, piece), piece)

    def inner(t):
        return pl.ds(t * piece, piece)

    far_base = col * 2 * per_dev
    near_base = (1 - col) * 2 * per_dev

    def walker_across(w, t):
        at = part(vec, t)
        return remote(walkers.at[w, at], partner.at[w, at], x_send.at[w, t], x_sem.at[w, t], across)

    def walker_z(w, t):
        return remote(partner.at[w, part(vec, t)], cand[t].at[far_base + w],
                      z_send.at[w, t], z_sem.at[w, t], z_to)

    def own_cand(w, t):
        return pltpu.make_async_copy(
            walkers.at[w, part(vec, t)], cand[t].at[per_dev + w], local_sem.at[w, t])

    def near_cand(w, t):
        return pltpu.make_async_copy(
            partner.at[w, part(vec, t)], cand[t].at[near_base + w], local_sem.at[w, PARTS + t])

    def walker_y(w, t):
        at = part(vec, t)
        return remote(partner.at[w, at], partner.at[w, at], y_send.at[w, t], y_sem.at[w, t], over)

    def walker_mate(w, t):
        at = part(vec, t)
        return remote(partner.at[w, at], partner.at[w, at], d_send.at[w, t], d_sem.at[w, t], mate)

    def walker_relay(w, t):
        at = part(far_vec, t)
        return remote(partner.at[w, at], partner.at[w, at], r_send.at[w, t], r_sem.at[w, t], mate)

    def slot_y(s, t):
        return remote(sel.at[s, inner(t)], branched.at[s, part(vec, t)], by_send.at[s, t], by_sem.at[s, t], over)

    def slot_mate(s, t):
        return remote(sel.at[s, inner(t)], branched.at[s, part(vec, t)], bd_send.at[s, t], bd_sem.at[s, t], mate)

    def slot_relay(s, t):
        at = part(far_vec, t)
        return remote(branched.at[s, at], branched.at[s, at], br_send.at[s, t], br_sem.at[s, t], mate)

    def slot_self(s, t):
        return pltpu.make_async_copy(sel.at[s, inner(t)], branched.at[s, part(vec, t)], self_sem.at[s, t])

    def each(lo, hi, f):
        def body(k, carry):
            f(k)
            return carry
        lax.fori_loop(lo, hi, body, 0)

    for w, t in pieces:
        own_cand(w, t).start()

    @pl.when(hub)
    def _():
        def start(k):
            own_to_home(k).start()

            @pl.when(k < AHEAD)
            def _():
                own_to_mate(k).start()

        for w, t in pieces:
            walker_across(w, t).start()
        each(0, chunks, start)

    @pl.when(jnp.logical_not(hub))
    def _():
        at = 0
        for n, (w, t) in enumerate(pieces):
            cut = min(QUEUE[min(n, len(QUEUE) - 1)], chunks)
            each(at, cut, lambda k: own_across(k).start())
            walker_across(w, t).start()
            at = cut
        each(at, chunks, lambda k: own_across(k).start())

    for w in range(per_dev):
        pltpu.make_async_copy(walkers.at[w], state.at[w], load_sem.at[w]).start()

    last = rows - 1
    here = flags[0] == 1
    below_or_here = flags[1] == 1
    from_home = flags[2] == 1

    def step(i):
        @pl.when(i < chunks)
        def _():
            @pl.when(hub)
            def _():
                own_across(i).wait_recv()
                away_to_mate(i).start()

                @pl.when(i + AHEAD < chunks)
                def _():
                    own_to_mate(i + AHEAD).start()

                own_to_home(i).wait()

            @pl.when(jnp.logical_not(hub))
            def _():
                own_to_mate(i).wait_recv()
                away_to_mate(i).wait_recv()

            own[i] = jnp.where(from_home, home[i], away[i])

        ku = i - SKEW * row
        kd = i - SKEW * (last - row)

        @pl.when(jnp.logical_and(ku >= 0, ku < chunks))
        def _():
            @pl.when(row == 0)
            def _():
                up[ku] = own[ku]

            @pl.when(row > 0)
            def _():
                send_up(ku).wait_recv()
                up[ku] = jnp.where(here, own[ku], up[ku])

            @pl.when(row < last)
            def _():
                send_up(ku).start()

        @pl.when(jnp.logical_and(kd >= 0, kd < chunks))
        def _():
            @pl.when(row == last)
            def _():
                down[kd] = own[kd]

            @pl.when(row < last)
            def _():
                send_down(kd).wait_recv()
                down[kd] = jnp.where(here, own[kd], down[kd])

            @pl.when(row > 0)
            def _():
                send_down(kd).start()

    def arrive(w, t):
        walker_across(w, t).wait_recv()
        walker_z(w, t).start()
        walker_y(w, t).start()
        walker_mate(w, t).start()
        near_cand(w, t).start()

    lines = 16

    def select(t):
        for w in range(per_dev):
            own_cand(w, t).wait()
            near_cand(w, t).wait()
            walker_z(w, t).wait_recv()
        for s in range(per_dev):
            index = slots[s]

            def pick(n, s=s, index=index):
                at = pl.ds(pl.multiple_of(t * piece + n * lines, lines), lines)
                sel[s, at, :] = cand[t][index, pl.ds(pl.multiple_of(n * lines, lines), lines), :]

            each(0, piece // lines, pick)
            slot_y(s, t).start()
            slot_mate(s, t).start()
            slot_self(s, t).start()

    def pass_on(w, t):
        walker_y(w, t).wait_recv()
        walker_relay(w, t).start()

    def pass_slots(t):
        for s in range(per_dev):
            slot_y(s, t).wait_recv()
            slot_relay(s, t).start()

    events = []
    for times, role in ((LEAF, jnp.logical_not(hub)), (HUB, hub)):
        for n, (w, t) in enumerate(pieces):
            n = min(n, len(times[0]) - 1)
            events.append((times[0][n], role, functools.partial(arrive, w, t)))
            events.append((times[1][n], role, functools.partial(pass_on, w, t)))
        for t in range(PARTS):
            events.append((times[2][t], role, functools.partial(select, t)))
            events.append((times[3][t], role, functools.partial(pass_slots, t)))
    events.sort(key=lambda event: event[0])

    def run(event):
        @pl.when(event[1])
        def _():
            event[2]()

    total = chunks + SKEW * last
    at = 0
    for event in events:
        if event[0] < 200:
            cut = min(event[0], total)
            if cut > at:
                each(at, cut, step)
                at = cut
            run(event)
    each(at, total, step)

    def finish(k):
        matrix[pl.ds(pl.multiple_of(k * depth, depth), depth), :] = jnp.where(below_or_here, up[k], down[k])

    each(0, chunks, finish)

    for w, t in pieces:
        walker_mate(w, t).wait_recv()
        walker_relay(w, t).wait_recv()

    def load(i):
        return pltpu.make_async_copy(partner.at[i], state.at[i], load_sem.at[i])

    sub = lax.broadcasted_iota(jnp.int32, result.shape, 0)
    lane = lax.broadcasted_iota(jnp.int32, result.shape, 1)
    result[...] = jnp.zeros_like(result)

    def compute(i):
        slot = lax.rem(i, per_dev)
        load(slot).wait()
        for n, value in enumerate(walker_values(matrix, state.at[slot])):
            result[...] = jnp.where(jnp.logical_and(sub == i, lane == n), value, result[...])

        @pl.when(i < per_dev)
        def _():
            load(slot).start()

    each(0, 2 * per_dev, compute)

    def tell(n):
        target, where = readers[n]
        return remote(result, table.at[where], t_send.at[n], t_sem.at[where], target)

    for n in range(len(readers)):
        tell(n).start()

    for event in events:
        if event[0] >= 200:
            run(event)

    table[place] = result[...]

    @pl.when(hub)
    def _():
        def ended(k):
            own_to_mate(k).wait_send()
            away_to_mate(k).wait_send()
        each(0, chunks, ended)

    @pl.when(jnp.logical_not(hub))
    def _():
        each(0, chunks, lambda k: own_across(k).wait_send())

    @pl.when(row < last)
    def _():
        each(0, chunks, lambda k: send_up(k).wait_send())

    @pl.when(row > 0)
    def _():
        each(0, chunks, lambda k: send_down(k).wait_send())

    for w, t in pieces:
        walker_across(w, t).wait_send()
        walker_z(w, t).wait_send()
        walker_y(w, t).wait_send()
        walker_mate(w, t).wait_send()
        walker_relay(w, t).wait_send()
    for n in range(len(readers)):
        tell(n).wait_send()

    for j in range(1, n_vec):
        v = lax.rem(vec + j, n_vec)
        remote(result, table.at[0], t_send.at[0], t_sem.at[col * n_vec + v], mate).wait_recv()
    for j in range(n_vec):
        remote(result, table.at[0], t_send.at[0], t_sem.at[(1 - col) * n_vec + j], mate).wait_recv()
    for j in range(2 * n_vec):
        remote(result, table.at[0], t_send.at[0], t_sem.at[2 * n_vec + j], mate).wait_recv()

    for t in range(PARTS):
        for s in range(per_dev):
            slot_y(s, t).wait_send()
            slot_mate(s, t).wait()
            slot_relay(s, t).wait()
            slot_self(s, t).wait()


def step_all(n_walk, n_vec, flags, slots, chol, walkers):
    per_dev, height, width = walkers.shape
    electrons, orbitals = chol.shape[2:]
    chunks = CHUNKS if electrons % (CHUNKS * 16) == 0 else 1
    depth = electrons // chunks
    big = pltpu.VMEM((chunks, depth, orbitals), chol.dtype)
    dma = pltpu.SemaphoreType.DMA
    any_spec = pl.BlockSpec(memory_space=pl.ANY)
    smem = pl.BlockSpec(memory_space=pltpu.SMEM)
    same = jax.ShapeDtypeStruct(walkers.shape, walkers.dtype)
    piece_sem = dma((per_dev, PARTS))
    return pl.pallas_call(
        functools.partial(step_kernel, n_walk, n_vec),
        out_shape=(jax.ShapeDtypeStruct((4 * n_vec, 8, 128), jnp.float32), same, same),
        in_specs=[smem, smem, any_spec, any_spec],
        out_specs=(pl.BlockSpec(memory_space=pltpu.VMEM), any_spec, any_spec),
        scratch_shapes=[
            big, big, big, big, big,
            pltpu.VMEM((3 * per_dev, height // n_vec // PARTS, width), walkers.dtype),
            pltpu.VMEM((3 * per_dev, height // n_vec // PARTS, width), walkers.dtype),
            pltpu.VMEM((per_dev, height // n_vec, width), walkers.dtype),
            pltpu.VMEM((electrons, orbitals), chol.dtype),
            pltpu.VMEM((per_dev, height, width), walkers.dtype),
            pltpu.VMEM((8, 128), jnp.float32),
        ] + [dma((chunks,))] * 9 + [piece_sem] * 4 + [dma((per_dev, 2 * PARTS))]
        + [piece_sem] * 13 + [dma((per_dev,)), dma((4 * n_vec - 1,)), dma((4 * n_vec,))],
        compiler_params=pltpu.CompilerParams(
            collective_id=0, has_side_effects=True, vmem_limit_bytes=60 * 1024 * 1024),
        name="step_all",
    )(flags, slots, chol, walkers)


def shards(n_walk, n_vec, walkers, chol, owners, branch_src):
    per_dev = walkers.shape[0]
    walk, vec = lax.axis_index("walk"), lax.axis_index("vec")
    row, col, low = walk // 2, walk % 2, vec % 2
    swap = [(i, i + 1 - 2 * (i % 2)) for i in range(n_vec)]
    mate_roots = lax.ppermute(owners[0], "vec", swap)
    roots = jnp.where(low == col, owners[0], mate_roots)
    root = jnp.take(roots, low)
    flags = jnp.stack([root // 2 == row, root // 2 <= row, root % 2 == col]).astype(jnp.int32)
    total = per_dev * n_walk
    relative = ((branch_src - (walk - 1) * per_dev + total) % total).astype(jnp.int32)
    table, _, branched = step_all(n_walk, n_vec, flags, relative, chol, walkers)
    table = table[:, :2 * per_dev, :4].reshape(2, 2, n_vec // 2, 2, 2, per_dev, 4)
    even, odd = table[:, 0], table[:, 1]
    first = jnp.stack([even[:, :, :, 0], odd[:, :, :, 1]], axis=2)
    second = jnp.stack([even[:, :, :, 1], odd[:, :, :, 0]], axis=2)
    both = jnp.stack([first, second], axis=1)
    both = jnp.transpose(both, (0, 1, 5, 2, 3, 4, 6)).reshape(4 * per_dev, n_vec, 2, 4)
    side = relative // per_dev
    block = jnp.where(side == 1, col, jnp.where(side == 2 * (1 - col), 1 - col, 3 - col))
    chosen = jnp.take(both, block * per_dev + relative % per_dev, axis=0)
    bias = lax.dynamic_slice_in_dim(chosen, vec, 1, axis=1)[:, 0, :, :2]
    energy = -0.5 * jnp.sum(chosen[..., 2:], axis=(1, 2))
    return (branched, bias, energy)


def solution(mesh):
    n_walk, n_vec = mesh.shape["walk"], mesh.shape["vec"]
    return jax.shard_map(
        functools.partial(shards, n_walk, n_vec),
        mesh=mesh,
        in_specs=(P("walk", None, None), P("vec", "walk", None, None), P("vec", None), P("walk")),
        out_specs=(P("walk", None, None), P("walk", "vec", None), P("walk", None)),
        check_vma=False,
    )
```

profile of v0, /device:TPU:0, one launch (start us, length us, event | category | flops | bytes accessed | tf_op | source)
XLA Modules:
  0.0 170.5 jit_solution(2825253945605552678)
XLA Ops:
  0.6 0.6 collective-permute-start
  1.2 1.2 compare_and_fusion
  2.4 0.0 collective-permute-done
  2.4 0.7 broadcast_select_fusion.1
  3.1 0.6 dynamic-slice.2
  4.3 0.6 add_convert_fusion.flags
  4.9 156.0 %step_all.1 = (f32[16,8,128]{2,1,0:T(8,128)}, bf16[2,2432,768]{2,1,0:T(8,128)(2,1)}, bf16[2,2432,768]{2,1,0:T(8,128)(2,1)}) custom-call(s32[3]{0:T(128)} %add_convert_fusion.flags, s32[2]{0:T(128)} %get-tuple-element.20.slots, bf16[1,1,384,4096]{3,2,1,0:T(8,128)(2,1)} %chol.1, bf16[2,2432,768]{2,1,0:T(8,128)(2,1)} %walkers.1), custom_call_target="tpu_custom_call" | custom-call | tf_op jit(solution)/shard_map/step_all/pallas_call | solution.py:423
  160.9 0.8 slice.27
  161.9 0.6 gather_fusion
  162.4 0.1 broadcast_select_fusion
  162.5 0.1 slice_reduce_fusion
  162.6 0.6 constant_dynamic-slice_fusion
  163.2 0.6 broadcast_multiply_fusion
  163.8 6.7 %copy.22 = bf16[2,2432,768]{2,1,0:T(8,128)(2,1)} copy(bf16[2,2432,768]{2,1,0:T(8,128)(2,1)} %get-tuple-element.32) | data formatting | bytes 14942208
  (8 shorter events, 0.1 us)
Async XLA Ops:
  0.6 1.8 %collective-permute-start = (s32[2]{0:T(128)}, s32[2]{0:T(128)S(1)}, u32[]{:S(2)}, u32[]{:S(2)}) collective-permute-start(s32[2]{0:T(128)} %bitcast.35), channel_id=1, source_target_pairs={{0,1},{1,0},{2,3},{3,2},{4,5},{5,4},{6,7},{7,6},{8,9},{9,8},{10,11... | collective-permute-start | bytes 32 | tf_op jit(solution)/shard_map/ppermute | solution.py:449
where the time goes:
time: 171 us; the launch traced here: 170 us
  Pallas kernels  156 us (91%)
  local copies, waits for them, and re-layouts  9.32 us (5%)
  other arithmetic  3.22 us (2%)
    pallas_call x1, Pallas kernels, step_all(): pl.pallas_call(functools.partial(step_kernel, n_walk, n_vec), out_shape=(...  156 us
    unnamed x1, local copies, waits for them, and re-layouts  6.69 us
  transfers between devices with their start and end apart: 1, of which 0 were waited for; matrix products, arithmetic and copies ran while one was open for 1% of the time, Pallas kernels for 0%

commit v1 on v0

v1 whole, which is shorter than its diff:
```python
import functools

import jax
import jax.numpy as jnp
from jax import lax
from jax.experimental import pallas as pl
from jax.experimental.pallas import tpu as pltpu
from jax.sharding import PartitionSpec as P

MESH = pl.DeviceIdType.MESH
LANES = 128
DEEP = 4
UNIT = 32
GROUP = 2
SKEW = 2
AHEAD = 3
X_SLOW = (16, 100)
X_FAST = 2
X_HUB = (16, 17, 18, 19, 20, 21, 23, 24, 25, 25)
X_LEAF = (3, 5, 7, 8, 10, 11, 12, 14, 15, 16)
Y_LAG = 3
LOAD_LAG = 2
CATCH_UP = 1
Z_HUB = (16, 3, 4)
Z_LEAF = (3, 5, 9)
Z_LAG = 3
Z_LAG_Y = 3
NEAR = 38
SPAN = 8


def flip(index):
    return index + 1 - 2 * lax.rem(index, 2)


def clip(value, low, high):
    return jnp.minimum(jnp.maximum(value, low), high)


def step_kernel(
    n_walk, n_vec, flags, chol, walkers, table, partner, beyond,
    home, away, up, down, mat, state, acc, result,
    home_sem, away_sem, up_sem, down_sem,
    mate_send, across_send, relay_send, up_send, down_send,
    x_send, y_send, d_send, r_send, z_send, zy_send, zd_send, zr_send,
    x_sem, y_sem, d_sem, r_sem, z_sem, zy_sem, zd_sem, zr_sem,
    load_sem, t_send, t_sem,
):
    walk, vec = lax.axis_index("walk"), lax.axis_index("vec")
    rows = n_walk // 2
    last = rows - 1
    row, col = walk // 2, lax.rem(walk, 2)
    low = lax.rem(vec, 2)
    hub = low == col
    leaf = jnp.logical_not(hub)
    pieces, electrons = home.shape[0], home.shape[1]
    blocks = pieces // DEEP
    per_dev = walkers.shape[0]
    quarter = walkers.shape[1] // n_vec
    units = quarter // UNIT
    groups = [(first, min(GROUP, units - first)) for first in range(0, units, GROUP)]
    ends = [first + size for first, size in groups]
    flip_walk, flip_vec = flip(walk), flip(vec)
    far_vec = lax.rem(vec + 2, n_vec)
    z_next = lax.rem(row + 1 - 2 * col + rows, rows)
    z_to = {"walk": z_next * 2 + col, "vec": vec}
    across = {"walk": flip_walk, "vec": vec}
    mate = {"walk": walk, "vec": flip_vec}
    over = {"walk": walk, "vec": far_vec}
    above = {"walk": walk + 2, "vec": vec}
    below = {"walk": walk - 2, "vec": vec}
    row_up, row_down = lax.rem(row + 1, rows), lax.rem(row + rows - 1, rows)

    place = col * n_vec + vec
    readers = [({"walk": walk, "vec": lax.rem(vec + j, n_vec)}, place) for j in range(1, n_vec)]
    readers += [({"walk": flip_walk, "vec": lax.rem(vec + j, n_vec)}, place) for j in range(n_vec)]
    readers += [({"walk": row_up * 2, "vec": lax.rem(vec + j, n_vec)}, place + 2 * n_vec) for j in range(n_vec)]
    readers += [({"walk": row_down * 2 + 1, "vec": lax.rem(vec + j, n_vec)}, place + 2 * n_vec) for j in range(n_vec)]

    def each(lo, hi, f):
        def body(k, carry):
            f(k)
            return carry
        lax.fori_loop(lo, hi, body, 0)

    def remote(src, dst, send, recv, target):
        return pltpu.make_async_remote_copy(
            src_ref=src, dst_ref=dst, send_sem=send, recv_sem=recv,
            device_id=target, device_id_type=MESH)

    def chol_piece(k):
        b, j = lax.div(k, DEEP), lax.rem(k, DEEP)
        half = DEEP // 2
        at = b * half + jnp.where(j < half, j, j - half + blocks * half)
        return chol.at[0, 0, :, pl.ds(pl.multiple_of(at * LANES, LANES), LANES)]

    def own_to_home(k):
        return pltpu.make_async_copy(chol_piece(k), home.at[k], home_sem.at[k])

    def own_to_mate(k):
        return remote(chol_piece(k), home.at[k], mate_send, home_sem.at[k], mate)

    def own_across(k):
        return remote(chol_piece(k), away.at[k], across_send, away_sem.at[k], across)

    def away_to_mate(k):
        return remote(away.at[k], away.at[k], relay_send, away_sem.at[k], mate)

    def send_up(k):
        return remote(up.at[k], up.at[k], up_send, up_sem.at[k], above)

    def send_down(k):
        return remote(down.at[k], down.at[k], down_send, down_sem.at[k], below)

    def unit_rows(u):
        return pl.ds(pl.multiple_of(vec * quarter + u * UNIT, UNIT), UNIT)

    def x_unit(u):
        at = unit_rows(u)
        return remote(walkers.at[:, at], partner.at[:, at], x_send, x_sem.at[lax.div(u, GROUP)], across)

    def z_unit(u):
        at = unit_rows(u)
        return remote(partner.at[:, at], beyond.at[:, at], z_send, z_sem.at[lax.div(u, GROUP)], z_to)

    def group(buffer, n, index, send, recv, target):
        first, size = groups[n]
        at = pl.ds(pl.multiple_of(index * quarter + first * UNIT, UNIT), size * UNIT)
        return remote(buffer.at[:, at], buffer.at[:, at], send, recv.at[n], target)

    def load(w):
        src = walkers.at[w] if w < per_dev else partner.at[w - per_dev]
        return pltpu.make_async_copy(src, state.at[w], load_sem.at[w])

    for w in range(per_dev):
        load(w).start()

    @pl.when(hub)
    def _():
        each(0, pieces, lambda k: own_to_home(k).start())

    bar = pltpu.get_barrier_semaphore()
    for target in (
        [t for t, _ in readers[:2 * n_vec - 1]]
        + [{"walk": r * 2 + c, "vec": lax.rem(vec + j, n_vec)}
           for r in (row_up, row_down) for c in range(2) for j in range(n_vec)]
    ):
        pl.semaphore_signal(bar, inc=1, device_id=target, device_id_type=MESH)
    pl.semaphore_wait(bar, 6 * n_vec - 1)

    @pl.when(hub)
    def _():
        each(0, min(AHEAD, pieces), lambda k: own_to_mate(k).start())
        each(0, units, lambda u: x_unit(u).start())

    @pl.when(leaf)
    def _():
        def x_count(k):
            slow = lax.div(jnp.minimum(k, X_SLOW[0]), X_SLOW[1])
            return jnp.minimum(slow + jnp.maximum(k - X_SLOW[0], 0) * X_FAST, units)

        def start(k):
            own_across(k).start()
            each(x_count(k), x_count(k + 1), lambda u: x_unit(u).start())
        each(0, pieces, start)
        each(x_count(pieces), units, lambda u: x_unit(u).start())

    acc[...] = jnp.zeros_like(acc)

    here = flags[0] == 1
    below_or_here = flags[1] == 1
    from_home = flags[2] == 1
    total = pieces + SKEW * last
    depth = jnp.maximum(row, last - row)

    def sent(i):
        begin, gain, per = (jnp.where(hub, a, b) for a, b in zip(Z_HUB, Z_LEAF))
        return jnp.minimum(lax.div(jnp.maximum(i - begin, 0) * gain, per), units)

    def chain(i):
        @pl.when(i < pieces)
        def _():
            @pl.when(hub)
            def _():
                own_across(i).wait_recv()
                away_to_mate(i).start()

                @pl.when(i + AHEAD < pieces)
                def _():
                    own_to_mate(i + AHEAD).start()

                own_to_home(i).wait()

            @pl.when(leaf)
            def _():
                own_to_mate(i).wait_recv()
                away_to_mate(i).wait_recv()

        ku = i - SKEW * row
        kd = i - SKEW * (last - row)

        @pl.when(jnp.logical_and(ku >= 0, ku < pieces))
        def _():
            own = jnp.where(from_home, home[ku], away[ku])

            @pl.when(row == 0)
            def _():
                up[ku] = own

            @pl.when(row > 0)
            def _():
                send_up(ku).wait_recv()
                up[ku] = jnp.where(here, own, up[ku])

            @pl.when(row < last)
            def _():
                send_up(ku).start()

        @pl.when(jnp.logical_and(kd >= 0, kd < pieces))
        def _():
            own = jnp.where(from_home, home[kd], away[kd])

            @pl.when(row == last)
            def _():
                down[kd] = own

            @pl.when(row < last)
            def _():
                send_down(kd).wait_recv()
                down[kd] = jnp.where(here, own, down[kd])

            @pl.when(row > 0)
            def _():
                send_down(kd).start()

        done = i - SKEW * depth

        @pl.when(jnp.logical_and(done >= 0, done < pieces))
        def _():
            mat[done] = jnp.where(below_or_here, up[done], down[done])

    load_at = X_HUB[-1] + Y_LAG + LOAD_LAG

    def arrive(n):
        group(partner, n, vec, x_send, x_sem, across).wait_recv()
        group(partner, n, vec, y_send, y_sem, over).start()
        group(partner, n, vec, d_send, d_sem, mate).start()

    def pass_on(n):
        group(partner, n, far_vec, y_send, y_sem, over).wait_recv()
        group(partner, n, far_vec, r_send, r_sem, mate).start()

    def load_partner():
        for n in range(len(groups)):
            group(partner, n, vec, d_send, d_sem, mate).wait_recv()
            group(partner, n, vec, r_send, r_sem, mate).wait_recv()
        for w in range(per_dev):
            load(per_dev + w).start()

    def loaded(first):
        for w in range(per_dev):
            load(first + w).wait()

    def z_arrive(n):
        group(beyond, n, vec, z_send, z_sem, z_to).wait_recv()
        group(beyond, n, vec, zy_send, zy_sem, over).start()
        group(beyond, n, vec, zd_send, zd_sem, mate).start()

    def z_pass_on(n):
        group(beyond, n, far_vec, zy_send, zy_sem, over).wait_recv()
        group(beyond, n, far_vec, zr_send, zr_sem, mate).start()

    half = DEEP // 2
    wide = half * LANES

    def multiply(b, w):
        p = state[w, pl.ds(pl.multiple_of(b * wide, wide), wide), :]
        re = jnp.concatenate([mat[b * DEEP + j] for j in range(half)], axis=1)
        im = jnp.concatenate([mat[b * DEEP + half + j] for j in range(half)], axis=1)
        x = jnp.dot(re, p, preferred_element_type=jnp.float32)
        y = jnp.dot(im, p, preferred_element_type=jnp.float32)
        acc[w, :, :electrons] += x[:, :electrons] - y[:, electrons:]
        acc[w, :, electrons:] += x[:, electrons:] + y[:, :electrons]

    def products(i):
        e = i - SKEW * depth - (DEEP - 1)
        def own_count(e, w):
            return clip(lax.div(e + DEEP - w, DEEP), 0, blocks)

        def partner_count(i, w):
            e = i - SKEW * depth - (DEEP - 1)
            full = clip(lax.div(e + DEEP, DEEP), 0, blocks)
            return jnp.where(i > total, blocks, clip((i - load_at - 2) * CATCH_UP, 0, full))

        spans = [(own_count(e - 1, w), own_count(e, w)) for w in range(per_dev)]
        spans += [(partner_count(i - 1, w), partner_count(i, w)) for w in range(per_dev)]
        def some(w, carry):
            lo, hi = spans[-1]
            for v in range(len(spans) - 1):
                lo = jnp.where(w == v, spans[v][0], lo)
                hi = jnp.where(w == v, spans[v][1], hi)
            lax.fori_loop(lo, hi, lambda b, c: (multiply(b, w), c)[1], 0)
            return carry
        lax.fori_loop(0, len(spans), some, 0)

    sub = lax.broadcasted_iota(jnp.int32, result.shape, 0)
    lane = lax.broadcasted_iota(jnp.int32, result.shape, 1)
    result[...] = jnp.zeros_like(result)
    orbitals = blocks * wide

    def finish(w):
        o = state[w, orbitals:, :]
        m = acc[w].astype(jnp.bfloat16)
        u = jnp.dot(m[:, :electrons], o, preferred_element_type=jnp.float32)
        v = jnp.dot(m[:, electrons:], o, preferred_element_type=jnp.float32)
        g_re = u[:, :electrons] - v[:, electrons:]
        g_im = u[:, electrons:] + v[:, :electrons]
        t_re, t_im = g_re.T, g_im.T
        eye = (lax.broadcasted_iota(jnp.int32, g_re.shape, 0)
               == lax.broadcasted_iota(jnp.int32, g_re.shape, 1))
        values = [
            jnp.sum(jnp.where(eye, g_re, 0.0)),
            jnp.sum(jnp.where(eye, g_im, 0.0)),
            jnp.sum(g_re * t_re - g_im * t_im),
            2.0 * jnp.sum(g_re * t_im),
        ]
        for n, value in enumerate(values):
            result[...] = jnp.where(jnp.logical_and(sub == w, lane == n), value, result[...])

    def tell(n):
        target, where = readers[n]
        return remote(result, table.at[where], t_send.at[n], t_sem.at[where], target)

    def tell_all():
        for n in range(len(readers)):
            tell(n).start()

    events, rest = [], []
    for times, z_times, role in ((X_HUB, Z_HUB, hub), (X_LEAF, Z_LEAF, leaf)):
        late = []
        for n, end in enumerate(ends):
            at = times[min(n, len(times) - 1)]
            events.append((at, role, functools.partial(arrive, n)))
            events.append((at + Y_LAG, role, functools.partial(pass_on, n)))
            at = z_times[0] + -(-end * z_times[2] // z_times[1]) + Z_LAG
            for run, when in ((z_arrive, at), (z_pass_on, at + Z_LAG_Y)):
                if when < min(total, NEAR):
                    events.append((when, role, functools.partial(run, n)))
                else:
                    late.append((run, n))
        late.sort(key=lambda item: item[1] + (1 if item[0] is z_pass_on else 0))
        rest.append((role, late))
    events.append((load_at, None, functools.partial(load_partner)))
    events.append((load_at + 2, None, functools.partial(loaded, per_dev)))
    events.append((min(DEEP - 1 + SKEW * (rows // 2), total), None, functools.partial(loaded, 0)))

    def handle(start, stop):
        for role, late in rest:
            @pl.when(role)
            def _():
                for run, n in late[start:stop]:
                    run(n)

    after = [
        lambda: each(sent(total - 1), units, lambda u: z_unit(u).start()),
        functools.partial(handle, 0, 1),
        lambda: each(total, total + 2, products),
    ]
    for w in range(2 * per_dev):
        after.append(functools.partial(handle, w + 1, w + 2))
        after.append(functools.partial(finish, w))
    after.append(tell_all)
    after.append(functools.partial(handle, 2 * per_dev + 1, 10 * len(groups)))

    families = {}
    for when, role, run in events:
        families.setdefault((run.func, when // SPAN) if role is not None else None, []).append((when, role, run))

    def step(i):
        chain(i)
        each(sent(i - 1), sent(i), lambda u: z_unit(u).start())
        for members in families.values():
            times = [when for when, _, _ in members]

            @pl.when(jnp.logical_and(i >= min(times), i <= max(times)))
            def _():
                for when, role, run in members:
                    pl.when(i == when if role is None else jnp.logical_and(i == when, role))(run)
        products(i)

    each(0, total, step)
    for run in after:
        run()

    table[place] = result[...]

    for n in range(len(groups)):
        group(beyond, n, vec, zd_send, zd_sem, mate).wait_recv()
        group(beyond, n, vec, zr_send, zr_sem, mate).wait_recv()

    def all_sent(buffer, send, target):
        remote(buffer, buffer, send, t_sem.at[0], target).wait_send()

    @pl.when(hub)
    def _():
        all_sent(home, mate_send, mate)
        all_sent(away, relay_send, mate)

    @pl.when(leaf)
    def _():
        all_sent(away, across_send, across)

    @pl.when(row < last)
    def _():
        all_sent(up, up_send, above)

    @pl.when(row > 0)
    def _():
        all_sent(down, down_send, below)

    part = partner.at[:, pl.ds(pl.multiple_of(vec * quarter, UNIT), quarter)]
    for send, target in (
        (x_send, across), (y_send, over), (d_send, mate), (r_send, mate),
        (z_send, z_to), (zy_send, over), (zd_send, mate), (zr_send, mate),
    ):
        all_sent(part, send, target)

    for n in range(len(readers)):
        tell(n).wait_send()

    for j in range(1, n_vec):
        v = lax.rem(vec + j, n_vec)
        remote(result, table.at[0], t_send.at[0], t_sem.at[col * n_vec + v], mate).wait_recv()
    for j in range(n_vec):
        remote(result, table.at[0], t_send.at[0], t_sem.at[(1 - col) * n_vec + j], mate).wait_recv()
    for j in range(2 * n_vec):
        remote(result, table.at[0], t_send.at[0], t_sem.at[2 * n_vec + j], mate).wait_recv()


def step_all(n_walk, n_vec, flags, chol, walkers):
    per_dev, height, width = walkers.shape
    electrons, orbitals = chol.shape[2:]
    pieces = orbitals // LANES
    groups = -(-(height // n_vec // UNIT) // GROUP)
    big = pltpu.VMEM((pieces, electrons, LANES), chol.dtype)
    dma = pltpu.SemaphoreType.DMA
    any_spec = pl.BlockSpec(memory_space=pl.ANY)
    smem = pl.BlockSpec(memory_space=pltpu.SMEM)
    same = jax.ShapeDtypeStruct(walkers.shape, walkers.dtype)
    return pl.pallas_call(
        functools.partial(step_kernel, n_walk, n_vec),
        out_shape=(jax.ShapeDtypeStruct((4 * n_vec, 8, 128), jnp.float32), same, same),
        in_specs=[smem, any_spec, any_spec],
        out_specs=(pl.BlockSpec(memory_space=pltpu.VMEM), any_spec, any_spec),
        scratch_shapes=[
            big, big, big, big, big,
            pltpu.VMEM((2 * per_dev, height, width), walkers.dtype),
            pltpu.VMEM((2 * per_dev, electrons, width), jnp.float32),
            pltpu.VMEM((8, 128), jnp.float32),
        ] + [dma((pieces,))] * 4 + [dma] * 13 + [dma((groups,))] * 8
        + [dma((2 * per_dev,)), dma((4 * n_vec - 1,)), dma((4 * n_vec,))],
        compiler_params=pltpu.CompilerParams(
            collective_id=0, has_side_effects=True, vmem_limit_bytes=62 * 1024 * 1024),
        name="step_all",
    )(flags, chol, walkers)


BITS = 4


def branch_kernel(sources, walkers, partner, beyond, branched, held, in_sem, out_sem):
    per_dev, height = walkers.shape[:2]
    piece = height // BITS

    def rows(t):
        return pl.ds(t * piece, piece)

    def fetch(buffer, s, t):
        return pltpu.make_async_copy(
            buffer.at[lax.rem(sources[s], per_dev), rows(t)], held.at[s, rows(t)], in_sem.at[s, t])

    def put(s, t):
        return pltpu.make_async_copy(held.at[s, rows(t)], branched.at[s, rows(t)], out_sem.at[s, t])

    cases = [(s, t) for s in range(per_dev) for t in range(BITS)]
    for s in range(per_dev):
        for which, buffer in enumerate((walkers, partner, beyond)):
            @pl.when(lax.div(sources[s], per_dev) == which)
            def _():
                for t in range(BITS):
                    fetch(buffer, s, t).start()
    for s, t in cases:
        fetch(walkers, s, t).wait()
        put(s, t).start()
    for s, t in cases:
        put(s, t).wait()


def branch(sources, walkers, partner, beyond):
    per_dev = walkers.shape[0]
    dma = pltpu.SemaphoreType.DMA
    any_spec = pl.BlockSpec(memory_space=pl.ANY)
    return pl.pallas_call(
        branch_kernel,
        out_shape=jax.ShapeDtypeStruct(walkers.shape, walkers.dtype),
        in_specs=[pl.BlockSpec(memory_space=pltpu.SMEM), any_spec, any_spec, any_spec],
        out_specs=any_spec,
        scratch_shapes=[pltpu.VMEM(walkers.shape, walkers.dtype), dma((per_dev, BITS)), dma((per_dev, BITS))],
        compiler_params=pltpu.CompilerParams(vmem_limit_bytes=62 * 1024 * 1024),
        name="branch",
    )(sources, walkers, partner, beyond)


def shards(n_walk, n_vec, walkers, chol, owners, branch_src):
    per_dev = walkers.shape[0]
    walk, vec = lax.axis_index("walk"), lax.axis_index("vec")
    row, col, low = walk // 2, walk % 2, vec % 2
    swap = [(i, i + 1 - 2 * (i % 2)) for i in range(n_vec)]
    mate_roots = lax.ppermute(owners[0], "vec", swap)
    roots = jnp.where(low == col, owners[0], mate_roots)
    root = jnp.take(roots, low)
    flags = jnp.stack([root // 2 == row, root // 2 <= row, root % 2 == col]).astype(jnp.int32)
    total = per_dev * n_walk
    relative = ((branch_src - (walk - 1) * per_dev + total) % total).astype(jnp.int32)
    table, partner, beyond = step_all(n_walk, n_vec, flags, chol, walkers)
    table = table[:, :2 * per_dev, :4].reshape(2, 2, n_vec // 2, 2, 2, per_dev, 4)
    even, odd = table[:, 0], table[:, 1]
    first = jnp.stack([even[:, :, :, 0], odd[:, :, :, 1]], axis=2)
    second = jnp.stack([even[:, :, :, 1], odd[:, :, :, 0]], axis=2)
    both = jnp.stack([first, second], axis=1)
    both = jnp.transpose(both, (0, 1, 5, 2, 3, 4, 6)).reshape(4 * per_dev, n_vec, 2, 4)
    side = relative // per_dev
    block = jnp.where(side == 1, col, jnp.where(side == 2 * (1 - col), 1 - col, 3 - col))
    chosen = jnp.take(both, block * per_dev + relative % per_dev, axis=0)
    kind = jnp.where(side == 1, 0, jnp.where(side == 2 * (1 - col), 1, 2))
    branched = branch(kind * per_dev + relative % per_dev, walkers, partner, beyond)
    bias = lax.dynamic_slice_in_dim(chosen, vec, 1, axis=1)[:, 0, :, :2]
    energy = -0.5 * jnp.sum(chosen[..., 2:], axis=(1, 2))
    return (branched, bias, energy)


def solution(mesh):
    n_walk, n_vec = mesh.shape["walk"], mesh.shape["vec"]
    return jax.shard_map(
        functools.partial(shards, n_walk, n_vec),
        mesh=mesh,
        in_specs=(P("walk", None, None), P("vec", "walk", None, None), P("vec", None), P("walk")),
        out_specs=(P("walk", None, None), P("walk", "vec", None), P("walk", None)),
        check_vma=False,
    )
```

time: 171 us -> 173 us (1.012)
  Pallas kernels: 156 us -> 165 us
  local copies, waits for them, and re-layouts: 9.32 us -> 2.63 us
    pallas_call x0 -> x1, Pallas kernels: none -> 6.82 us  [branch(): pl.pallas_call(branch_kernel, out_shape=jax.ShapeDtypeStruct(walkers.shap...]
    unnamed x1 -> x0, local copies, waits for them, and re-layouts: 6.69 us -> none
    pallas_call x1, Pallas kernels: 156 us -> 158 us  [step_all(): pl.pallas_call(functools.partial(step_kernel, n_walk, n_vec), out_shape=(...]
where the time goes in v1:
time: 173 us
  Pallas kernels  165 us (95%)
  other arithmetic  3.25 us (2%)
  local copies, waits for them, and re-layouts  2.63 us (2%)
    pallas_call x1, Pallas kernels, step_all(): pl.pallas_call(functools.partial(step_kernel, n_walk, n_vec), out_shape=(...  158 us
    pallas_call x1, Pallas kernels, branch(): pl.pallas_call(branch_kernel, out_shape=jax.ShapeDtypeStruct(walkers.shap...  6.82 us
  transfers between devices with their start and end apart: 1, of which 0 were waited for; matrix products, arithmetic and copies ran while one was open for 1% of the time, Pallas kernels for 0%

profile of v1, /device:TPU:0, one launch (start us, length us, event | category | flops | bytes accessed | tf_op | source)
XLA Modules:
  0.0 173.1 jit_solution(2204878479053106972)
XLA Ops:
  0.6 0.6 collective-permute-start
  1.2 0.7 compare_and_fusion
  1.9 0.5 fusion.1.sources
  2.4 0.0 collective-permute-done
  2.4 0.7 broadcast_select_fusion.1
  3.1 0.6 dynamic-slice.2
  4.4 0.6 add_convert_fusion.flags
  5.0 158.5 %step_all.1 = (f32[16,8,128]{2,1,0:T(8,128)}, bf16[2,2432,768]{2,1,0:T(8,128)(2,1)}, bf16[2,2432,768]{2,1,0:T(8,128)(2,1)}) custom-call(s32[3]{0:T(128)} %add_convert_fusion.flags, bf16[1,1,384,4096]{3,2,1,0:T(8,128)(2,1)} %chol.1, bf16[2,2432,768]{2,1,0:T(8,128)(2,1)} %walkers.3), custom_call_target="tpu_custom_call" | custom-call | tf_op jit(solution)/shard_map/step_all/pallas_call | solution.py:450
  163.5 0.8 slice.27
  164.4 0.6 gather_fusion
  165.0 0.1 broadcast_select_fusion
  165.1 0.1 slice_reduce_fusion
  165.2 0.6 constant_dynamic-slice_fusion
  165.8 0.6 broadcast_multiply_fusion
  166.3 6.8 %branch.1 = bf16[2,2432,768]{2,1,0:T(8,128)(2,1)} custom-call(s32[2]{0:T(128)} %fusion.1.sources, bf16[2,2432,768]{2,1,0:T(8,128)(2,1)} %walkers.3, bf16[2,2432,768]{2,1,0:T(8,128)(2,1)} %get-tuple-element.6.partner, bf16[2,2432,768]{2,1,0:T(8,128)(2,1)} %get-tuple-element.7.beyond), custom_call_target="tpu_custom_call" | custom-call | tf_op jit(solution)/shard_map/branch/pallas_call | solution.py:503
  (8 shorter events, 0.1 us)
Async XLA Ops:
  0.6 1.8 %collective-permute-start = (s32[2]{0:T(128)}, s32[2]{0:T(128)S(1)}, u32[]{:S(2)}, u32[]{:S(2)}) collective-permute-start(s32[2]{0:T(128)} %bitcast.35), channel_id=1, source_target_pairs={{0,1},{1,0},{2,3},{3,2},{4,5},{5,4},{6,7},{7,6},{8,9},{9,8},{10,11... | collective-permute-start | bytes 32 | tf_op jit(solution)/shard_map/ppermute | solution.py:519

commit v2 on v1

--- a/solution.py
+++ b/solution.py
@@ -12,7 +12,7 @@
 DEEP = 4
 UNIT = 32
 GROUP = 2
-SKEW = 2
+SKEW = 3
 AHEAD = 3
 X_SLOW = (16, 100)
 X_FAST = 2
@@ -20,12 +20,18 @@
 X_LEAF = (3, 5, 7, 8, 10, 11, 12, 14, 15, 16)
 Y_LAG = 3
 LOAD_LAG = 2
-CATCH_UP = 1
-Z_HUB = (16, 3, 4)
-Z_LEAF = (3, 5, 9)
+CATCH_UP = 2
+Z_HUB = (16, 35)
+Z_LEAF = (5, 32)
 Z_LAG = 3
 Z_LAG_Y = 3
-NEAR = 38
+NEAR = 41
+RELAY = 22
+RELAY_LAG = 5
+DIRECT = (2, 1, 4)
+DIRECT_WRAP = 3
+WRAP_START = 8
+WRAP_STEPS = 4
 SPAN = 8
 
 
@@ -38,13 +44,13 @@
 
 
 def step_kernel(
-    n_walk, n_vec, flags, chol, walkers, table, partner, beyond,
-    home, away, up, down, mat, state, acc, result,
+    n_walk, n_vec, owners, chol, walkers, table, partner, beyond,
+    home, away, up, down, mat, hold, state, acc, result, note, told,
     home_sem, away_sem, up_sem, down_sem,
     mate_send, across_send, relay_send, up_send, down_send,
-    x_send, y_send, d_send, r_send, z_send, zy_send, zd_send, zr_send,
+    x_send, y_send, d_send, r_send, zy_send, zd_send, zr_send, z_send, direct_send, hold_send, hold_sem,
     x_sem, y_sem, d_sem, r_sem, z_sem, zy_sem, zd_sem, zr_sem,
-    load_sem, t_send, t_sem,
+    load_sem, note_send, note_sem, t_send, t_sem,
 ):
     walk, vec = lax.axis_index("walk"), lax.axis_index("vec")
     rows = n_walk // 2
@@ -63,6 +69,10 @@
     flip_walk, flip_vec = flip(walk), flip(vec)
     far_vec = lax.rem(vec + 2, n_vec)
     z_next = lax.rem(row + 1 - 2 * col + rows, rows)
+    order = jnp.where(col == 0, row, last - row)
+    order_own = last - order
+    z_own = lax.rem(row + 2 * col - 1 + rows, rows)
+    direct_to = {"walk": z_own * 2 + col, "vec": vec}
     z_to = {"walk": z_next * 2 + col, "vec": vec}
     across = {"walk": flip_walk, "vec": vec}
     mate = {"walk": walk, "vec": flip_vec}
@@ -121,7 +131,29 @@
 
     def z_unit(u):
         at = unit_rows(u)
-        return remote(partner.at[:, at], beyond.at[:, at], z_send, z_sem.at[lax.div(u, GROUP)], z_to)
+        return remote(partner.at[:, at], beyond.at[:, at], z_send.at[u], z_sem.at[lax.div(u, GROUP)], z_to)
+
+    def direct_unit(u):
+        at = unit_rows(u)
+        return remote(walkers.at[:, at], hold.at[u], direct_send.at[u], hold_sem.at[u], direct_to)
+
+    def relay_unit(u):
+        at = unit_rows(u)
+        return remote(hold.at[u], beyond.at[:, at], hold_send.at[u], z_sem.at[lax.div(u, GROUP)], across)
+
+    def direct_count(position):
+        return jnp.where(position == last, DIRECT_WRAP,
+                         jnp.minimum(DIRECT[0] + DIRECT[1] * position, DIRECT[2]))
+
+    def relay_all():
+        def one(u):
+            direct_unit(u).wait_recv()
+            relay_unit(u).start()
+        each(0, direct_count(lax.rem(order_own + last, rows)), one)
+
+    def direct_sent(i):
+        paced = clip(lax.div(i - WRAP_START + WRAP_STEPS, WRAP_STEPS), 0, DIRECT_WRAP)
+        return jnp.where(order_own == last, paced, direct_count(order_own))
 
     def group(buffer, n, index, send, recv, target):
         first, size = groups[n]
@@ -138,6 +170,22 @@
     @pl.when(hub)
     def _():
         each(0, pieces, lambda k: own_to_home(k).start())
+
+    def code_of(root):
+        here = (lax.div(root, 2) == row).astype(jnp.float32)
+        under = (lax.div(root, 2) <= row).astype(jnp.float32)
+        at_home = (lax.rem(root, 2) == col).astype(jnp.float32)
+        return here + 2.0 * under + 4.0 * at_home
+
+    code_mate = jnp.where(low == 0, code_of(owners[0, 1]), code_of(owners[0, 0]))
+    code_own = jnp.where(low == 0, code_of(owners[0, 0]), code_of(owners[0, 1]))
+    note[...] = jnp.full(note.shape, code_mate, jnp.float32)
+
+    @pl.when(hub)
+    def _():
+        told[...] = jnp.full(told.shape, code_own, jnp.float32)
+
+    send_note = remote(note, told, note_send, note_sem, mate)
 
     bar = pltpu.get_barrier_semaphore()
     for target in (
@@ -148,8 +196,11 @@
         pl.semaphore_signal(bar, inc=1, device_id=target, device_id_type=MESH)
     pl.semaphore_wait(bar, 6 * n_vec - 1)
 
+    each(0, direct_sent(0), lambda u: direct_unit(u).start())
+
     @pl.when(hub)
     def _():
+        send_note.start()
         each(0, min(AHEAD, pieces), lambda k: own_to_mate(k).start())
         each(0, units, lambda u: x_unit(u).start())
 
@@ -167,15 +218,26 @@
 
     acc[...] = jnp.zeros_like(acc)
 
-    here = flags[0] == 1
-    below_or_here = flags[1] == 1
-    from_home = flags[2] == 1
+    @pl.when(leaf)
+    def _():
+        send_note.wait_recv()
+
+    code = jnp.max(told[...])
+    from_home = code >= 4.0
+    code = jnp.where(from_home, code - 4.0, code)
+    below_or_here = code >= 2.0
+    here = jnp.where(below_or_here, code - 2.0, code) >= 1.0
     total = pieces + SKEW * last
     depth = jnp.maximum(row, last - row)
 
+    skip = direct_count(order)
+
     def sent(i):
-        begin, gain, per = (jnp.where(hub, a, b) for a, b in zip(Z_HUB, Z_LEAF))
-        return jnp.minimum(lax.div(jnp.maximum(i - begin, 0) * gain, per), units)
+        gone = jnp.where(
+            hub,
+            lax.div(jnp.maximum(i - Z_HUB[0], 0) * (units - skip), Z_HUB[1] - Z_HUB[0]),
+            lax.div(jnp.maximum(i - Z_LEAF[0], 0) * (units - skip), Z_LEAF[1] - Z_LEAF[0]))
+        return jnp.minimum(skip + gone, units)
 
     def chain(i):
         @pl.when(i < pieces)
@@ -262,7 +324,7 @@
             load(first + w).wait()
 
     def z_arrive(n):
-        group(beyond, n, vec, z_send, z_sem, z_to).wait_recv()
+        group(beyond, n, vec, zy_send, z_sem, z_to).wait_recv()
         group(beyond, n, vec, zy_send, zy_sem, over).start()
         group(beyond, n, vec, zd_send, zd_sem, mate).start()
 
@@ -342,7 +404,11 @@
             at = times[min(n, len(times) - 1)]
             events.append((at, role, functools.partial(arrive, n)))
             events.append((at + Y_LAG, role, functools.partial(pass_on, n)))
-            at = z_times[0] + -(-end * z_times[2] // z_times[1]) + Z_LAG
+            fewest = min(DIRECT[0], DIRECT_WRAP)
+            span = z_times[1] - z_times[0]
+            at = z_times[0] + -(-max(end - fewest, 0) * span // (units - fewest)) + Z_LAG
+            if groups[n][0] < max(DIRECT[2], DIRECT_WRAP):
+                at = max(at, RELAY + RELAY_LAG)
             for run, when in ((z_arrive, at), (z_pass_on, at + Z_LAG_Y)):
                 if when < min(total, NEAR):
                     events.append((when, role, functools.partial(run, n)))
@@ -350,6 +416,7 @@
                     late.append((run, n))
         late.sort(key=lambda item: item[1] + (1 if item[0] is z_pass_on else 0))
         rest.append((role, late))
+    events.append((RELAY, None, functools.partial(relay_all)))
     events.append((load_at, None, functools.partial(load_partner)))
     events.append((load_at + 2, None, functools.partial(loaded, per_dev)))
     events.append((min(DEEP - 1 + SKEW * (rows // 2), total), None, functools.partial(loaded, 0)))
@@ -378,7 +445,6 @@
 
     def step(i):
         chain(i)
-        each(sent(i - 1), sent(i), lambda u: z_unit(u).start())
         for members in families.values():
             times = [when for when, _, _ in members]
 
@@ -386,6 +452,8 @@
             def _():
                 for when, role, run in members:
                     pl.when(i == when if role is None else jnp.logical_and(i == when, role))(run)
+        each(jnp.where(i == 0, direct_sent(0), direct_sent(i - 1)), direct_sent(i), lambda u: direct_unit(u).start())
+        each(sent(i - 1), sent(i), lambda u: z_unit(u).start())
         products(i)
 
     each(0, total, step)
@@ -403,6 +471,7 @@
 
     @pl.when(hub)
     def _():
+        send_note.wait_send()
         all_sent(home, mate_send, mate)
         all_sent(away, relay_send, mate)
 
@@ -421,9 +490,13 @@
     part = partner.at[:, pl.ds(pl.multiple_of(vec * quarter, UNIT), quarter)]
     for send, target in (
         (x_send, across), (y_send, over), (d_send, mate), (r_send, mate),
-        (z_send, z_to), (zy_send, over), (zd_send, mate), (zr_send, mate),
+        (zy_send, over), (zd_send, mate), (zr_send, mate),
     ):
         all_sent(part, send, target)
+
+    each(skip, units, lambda u: z_unit(u).wait_send())
+    each(0, direct_count(order_own), lambda u: direct_unit(u).wait_send())
+    each(0, direct_count(lax.rem(order_own + last, rows)), lambda u: relay_unit(u).wait_send())
 
     for n in range(len(readers)):
         tell(n).wait_send()
@@ -437,11 +510,12 @@
         remote(result, table.at[0], t_send.at[0], t_sem.at[2 * n_vec + j], mate).wait_recv()
 
 
-def step_all(n_walk, n_vec, flags, chol, walkers):
+def step_all(n_walk, n_vec, owners, chol, walkers):
     per_dev, height, width = walkers.shape
     electrons, orbitals = chol.shape[2:]
     pieces = orbitals // LANES
-    groups = -(-(height // n_vec // UNIT) // GROUP)
+    units = height // n_vec // UNIT
+    groups = -(-units // GROUP)
     big = pltpu.VMEM((pieces, electrons, LANES), chol.dtype)
     dma = pltpu.SemaphoreType.DMA
     any_spec = pl.BlockSpec(memory_space=pl.ANY)
@@ -454,89 +528,104 @@
         out_specs=(pl.BlockSpec(memory_space=pltpu.VMEM), any_spec, any_spec),
         scratch_shapes=[
             big, big, big, big, big,
+            pltpu.VMEM((max(DIRECT[2], DIRECT_WRAP), per_dev, UNIT, width), walkers.dtype),
             pltpu.VMEM((2 * per_dev, height, width), walkers.dtype),
             pltpu.VMEM((2 * per_dev, electrons, width), jnp.float32),
             pltpu.VMEM((8, 128), jnp.float32),
-        ] + [dma((pieces,))] * 4 + [dma] * 13 + [dma((groups,))] * 8
-        + [dma((2 * per_dev,)), dma((4 * n_vec - 1,)), dma((4 * n_vec,))],
+            pltpu.VMEM((8, 128), jnp.float32),
+            pltpu.VMEM((8, 128), jnp.float32),
+        ] + [dma((pieces,))] * 4 + [dma] * 12 + [dma((units,))] * 4 + [dma((groups,))] * 8
+        + [dma((2 * per_dev,)), dma, dma, dma((4 * n_vec - 1,)), dma((4 * n_vec,))],
         compiler_params=pltpu.CompilerParams(
             collective_id=0, has_side_effects=True, vmem_limit_bytes=62 * 1024 * 1024),
         name="step_all",
-    )(flags, chol, walkers)
+    )(owners, chol, walkers)
 
 
 BITS = 4
 
 
-def branch_kernel(sources, walkers, partner, beyond, branched, held, in_sem, out_sem):
+def branch_kernel(
+    n_walk, n_vec, slots, walkers, partner, beyond, table,
+    branched, bias, energy, held, facts, in_sem, out_sem, t_sem,
+):
+    walk, vec = lax.axis_index("walk"), lax.axis_index("vec")
+    col = lax.rem(walk, 2)
     per_dev, height = walkers.shape[:2]
     piece = height // BITS
+    total = per_dev * n_walk
 
     def rows(t):
         return pl.ds(t * piece, piece)
 
-    def fetch(buffer, s, t):
-        return pltpu.make_async_copy(
-            buffer.at[lax.rem(sources[s], per_dev), rows(t)], held.at[s, rows(t)], in_sem.at[s, t])
+    def fetch(buffer, w, s, t):
+        return pltpu.make_async_copy(buffer.at[w, rows(t)], held.at[s, rows(t)], in_sem.at[s, t])
 
     def put(s, t):
         return pltpu.make_async_copy(held.at[s, rows(t)], branched.at[s, rows(t)], out_sem.at[s, t])
 
     cases = [(s, t) for s in range(per_dev) for t in range(BITS)]
+    picks = []
     for s in range(per_dev):
-        for which, buffer in enumerate((walkers, partner, beyond)):
-            @pl.when(lax.div(sources[s], per_dev) == which)
+        relative = lax.rem(slots[s] - (walk - 1) * per_dev + total, total)
+        side, w = lax.div(relative, per_dev), lax.rem(relative, per_dev)
+        mine, beside = side == 1, side == 2 * (1 - col)
+        far = jnp.logical_not(jnp.logical_or(mine, beside))
+        picks.append((w, jnp.where(far, 1, 0), jnp.where(mine, col, 1 - col)))
+        for wanted, buffer in ((mine, walkers), (beside, partner), (far, beyond)):
+            @pl.when(wanted)
             def _():
                 for t in range(BITS):
-                    fetch(buffer, s, t).start()
+                    fetch(buffer, w, s, t).start()
+    facts_in = pltpu.make_async_copy(table, facts, t_sem)
+    facts_in.start()
     for s, t in cases:
-        fetch(walkers, s, t).wait()
+        fetch(walkers, 0, s, t).wait()
         put(s, t).start()
+    facts_in.wait()
+
+    for s, (w, far, block) in enumerate(picks):
+        def value(v, g, lane):
+            sender = lax.rem(v, 2)
+            at = far * 2 * n_vec + sender * n_vec + lax.div(v, 2) * 2 + g
+            return facts[at, jnp.where(block == sender, 0, per_dev) + w, lane]
+
+        for g in range(2):
+            for part in range(2):
+                bias[s, g, part] = value(vec, g, part)
+        for part in range(2):
+            energy[s, part] = -0.5 * sum(value(jnp.int32(v), g, 2 + part) for v in range(n_vec) for g in range(2))
+
     for s, t in cases:
         put(s, t).wait()
 
 
-def branch(sources, walkers, partner, beyond):
+def branch(n_walk, n_vec, slots, walkers, partner, beyond, table):
     per_dev = walkers.shape[0]
     dma = pltpu.SemaphoreType.DMA
     any_spec = pl.BlockSpec(memory_space=pl.ANY)
+    smem = pl.BlockSpec(memory_space=pltpu.SMEM)
     return pl.pallas_call(
-        branch_kernel,
-        out_shape=jax.ShapeDtypeStruct(walkers.shape, walkers.dtype),
-        in_specs=[pl.BlockSpec(memory_space=pltpu.SMEM), any_spec, any_spec, any_spec],
-        out_specs=any_spec,
-        scratch_shapes=[pltpu.VMEM(walkers.shape, walkers.dtype), dma((per_dev, BITS)), dma((per_dev, BITS))],
+        functools.partial(branch_kernel, n_walk, n_vec),
+        out_shape=(
+            jax.ShapeDtypeStruct(walkers.shape, walkers.dtype),
+            jax.ShapeDtypeStruct((per_dev, 2, 2), jnp.float32),
+            jax.ShapeDtypeStruct((per_dev, 2), jnp.float32),
+        ),
+        in_specs=[smem, any_spec, any_spec, any_spec, any_spec],
+        out_specs=(any_spec, smem, smem),
+        scratch_shapes=[
+            pltpu.VMEM(walkers.shape, walkers.dtype), pltpu.SMEM(table.shape, table.dtype),
+            dma((per_dev, BITS)), dma((per_dev, BITS)), dma,
+        ],
         compiler_params=pltpu.CompilerParams(vmem_limit_bytes=62 * 1024 * 1024),
         name="branch",
-    )(sources, walkers, partner, beyond)
+    )(slots, walkers, partner, beyond, table)
 
 
 def shards(n_walk, n_vec, walkers, chol, owners, branch_src):
-    per_dev = walkers.shape[0]
-    walk, vec = lax.axis_index("walk"), lax.axis_index("vec")
-    row, col, low = walk // 2, walk % 2, vec % 2
-    swap = [(i, i + 1 - 2 * (i % 2)) for i in range(n_vec)]
-    mate_roots = lax.ppermute(owners[0], "vec", swap)
-    roots = jnp.where(low == col, owners[0], mate_roots)
-    root = jnp.take(roots, low)
-    flags = jnp.stack([root // 2 == row, root // 2 <= row, root % 2 == col]).astype(jnp.int32)
-    total = per_dev * n_walk
-    relative = ((branch_src - (walk - 1) * per_dev + total) % total).astype(jnp.int32)
-    table, partner, beyond = step_all(n_walk, n_vec, flags, chol, walkers)
-    table = table[:, :2 * per_dev, :4].reshape(2, 2, n_vec // 2, 2, 2, per_dev, 4)
-    even, odd = table[:, 0], table[:, 1]
-    first = jnp.stack([even[:, :, :, 0], odd[:, :, :, 1]], axis=2)
-    second = jnp.stack([even[:, :, :, 1], odd[:, :, :, 0]], axis=2)
-    both = jnp.stack([first, second], axis=1)
-    both = jnp.transpose(both, (0, 1, 5, 2, 3, 4, 6)).reshape(4 * per_dev, n_vec, 2, 4)
-    side = relative // per_dev
-    block = jnp.where(side == 1, col, jnp.where(side == 2 * (1 - col), 1 - col, 3 - col))
-    chosen = jnp.take(both, block * per_dev + relative % per_dev, axis=0)
-    kind = jnp.where(side == 1, 0, jnp.where(side == 2 * (1 - col), 1, 2))
-    branched = branch(kind * per_dev + relative % per_dev, walkers, partner, beyond)
-    bias = lax.dynamic_slice_in_dim(chosen, vec, 1, axis=1)[:, 0, :, :2]
-    energy = -0.5 * jnp.sum(chosen[..., 2:], axis=(1, 2))
-    return (branched, bias, energy)
+    table, partner, beyond = step_all(n_walk, n_vec, owners, chol, walkers)
+    return branch(n_walk, n_vec, branch_src, walkers, partner, beyond, table)
 
 
 def solution(mesh):

time: 173 us -> 153 us (0.88)
  Pallas kernels: 165 us -> 152 us
  other arithmetic: 3.25 us -> 0 us
  local copies, waits for them, and re-layouts: 2.63 us -> 0 us
    pallas_call x1, Pallas kernels: 158 us -> 145 us  [step_all(): pl.pallas_call(functools.partial(step_kernel, n_walk, n_vec), out_shape=(...]
  transfers between devices with their start and end apart: 1 -> 0, of which waited for: 0 -> 0; matrix products, arithmetic and copies ran while one was open for 1% -> 0% of each run, Pallas kernels for 0% -> 0%
where the time goes in v2:
time: 153 us
  Pallas kernels  152 us (99%)
    pallas_call x1, Pallas kernels, step_all(): pl.pallas_call(functools.partial(step_kernel, n_walk, n_vec), out_shape=(...  145 us
    pallas_call x1, Pallas kernels, branch(): pl.pallas_call(functools.partial(branch_kernel, n_walk, n_vec), out_shape...  7.45 us

profile of v2, /device:TPU:0, one launch (start us, length us, event | category | flops | bytes accessed | tf_op | source)
XLA Modules:
  0.0 153.1 jit_solution(14210413114908338063)
XLA Ops:
  0.6 145.0 %step_all.1 = (f32[16,8,128]{2,1,0:T(8,128)}, bf16[2,2432,768]{2,1,0:T(8,128)(2,1)}, bf16[2,2432,768]{2,1,0:T(8,128)(2,1)}) custom-call(s32[1,2]{1,0:T(1,128)} %owners.1, bf16[1,1,384,4096]{3,2,1,0:T(8,128)(2,1)} %chol.1, bf16[2,2432,768]{2,1,0:T(8,128)(2,1)} %walkers.3), custom_call_target="tpu_custom_call" | custom-call | tf_op jit(solution)/shard_map/step_all/pallas_call | solution.py:524
  145.6 7.5 %branch.1 = (bf16[2,2432,768]{2,1,0:T(8,128)(2,1)}, f32[2,2,2]{2,1,0:T(2,128)}, f32[2,2]{1,0:T(2,128)}) custom-call(s32[2]{0:T(128)} %slots.1, bf16[2,2432,768]{2,1,0:T(8,128)(2,1)} %walkers.3, bf16[2,2432,768]{2,1,0:T(8,128)(2,1)} %get-tuple-element.6.partner, bf16[2,2432,768]{2,1,0:T(8,128)(2,1)} %get-tuple-element.7.beyond, ...), custom_call_target="tpu_custom_call" | custom-call | tf_op jit(solution)/shard_map/branch/pallas_call | solution.py:608

commit v3 on v2

--- a/solution.py
+++ b/solution.py
@@ -13,7 +13,8 @@
 UNIT = 32
 GROUP = 2
 SKEW = 3
-AHEAD = 3
+AHEAD = 8
+BATCH = 4
 X_SLOW = (16, 100)
 X_FAST = 2
 X_HUB = (16, 17, 18, 19, 20, 21, 23, 24, 25, 25)
@@ -21,7 +22,7 @@
 Y_LAG = 3
 LOAD_LAG = 2
 CATCH_UP = 2
-Z_HUB = (16, 35)
+Z_HUB = (16, 33)
 Z_LEAF = (5, 32)
 Z_LAG = 3
 Z_LAG_Y = 3
@@ -30,8 +31,8 @@
 RELAY_LAG = 5
 DIRECT = (2, 1, 4)
 DIRECT_WRAP = 3
-WRAP_START = 8
-WRAP_STEPS = 4
+WRAP_START = 4
+WRAP_STEPS = 2
 SPAN = 8
 
 
@@ -49,8 +50,8 @@
     home_sem, away_sem, up_sem, down_sem,
     mate_send, across_send, relay_send, up_send, down_send,
     x_send, y_send, d_send, r_send, zy_send, zd_send, zr_send, z_send, direct_send, hold_send, hold_sem,
-    x_sem, y_sem, d_sem, r_sem, z_sem, zy_sem, zd_sem, zr_sem,
-    load_sem, note_send, note_sem, t_send, t_sem,
+    x_sem, y_sem, z_sem, zy_sem, d_sem, r_sem, zd_sem, zr_sem,
+    load_sem, keep_sem, note_send, note_sem, t_send, t_sem,
 ):
     walk, vec = lax.axis_index("walk"), lax.axis_index("vec")
     rows = n_walk // 2
@@ -105,10 +106,13 @@
         return chol.at[0, 0, :, pl.ds(pl.multiple_of(at * LANES, LANES), LANES)]
 
     def own_to_home(k):
-        return pltpu.make_async_copy(chol_piece(k), home.at[k], home_sem.at[k])
+        return pltpu.make_async_copy(chol_piece(k), home.at[k], home_sem.at[lax.div(k, BATCH)])
+
+    def home_batch(k):
+        return home.at[pl.ds(k, BATCH)]
 
     def own_to_mate(k):
-        return remote(chol_piece(k), home.at[k], mate_send, home_sem.at[k], mate)
+        return remote(chol_piece(k), home.at[k], mate_send, home_sem.at[lax.div(k, BATCH)], mate)
 
     def own_across(k):
         return remote(chol_piece(k), away.at[k], across_send, away_sem.at[k], across)
@@ -131,7 +135,7 @@
 
     def z_unit(u):
         at = unit_rows(u)
-        return remote(partner.at[:, at], beyond.at[:, at], z_send.at[u], z_sem.at[lax.div(u, GROUP)], z_to)
+        return remote(partner.at[:, at], beyond.at[:, at], z_send, z_sem.at[lax.div(u, GROUP)], z_to)
 
     def direct_unit(u):
         at = unit_rows(u)
@@ -158,34 +162,15 @@
     def group(buffer, n, index, send, recv, target):
         first, size = groups[n]
         at = pl.ds(pl.multiple_of(index * quarter + first * UNIT, UNIT), size * UNIT)
-        return remote(buffer.at[:, at], buffer.at[:, at], send, recv.at[n], target)
+        return remote(buffer.at[:, at], buffer.at[:, at], send, recv, target)
+
+    def quarter_of(buffer, send, recv):
+        at = pl.ds(pl.multiple_of(vec * quarter, UNIT), quarter)
+        return remote(buffer.at[:, at], buffer.at[:, at], send, recv, mate)
 
     def load(w):
         src = walkers.at[w] if w < per_dev else partner.at[w - per_dev]
         return pltpu.make_async_copy(src, state.at[w], load_sem.at[w])
-
-    for w in range(per_dev):
-        load(w).start()
-
-    @pl.when(hub)
-    def _():
-        each(0, pieces, lambda k: own_to_home(k).start())
-
-    def code_of(root):
-        here = (lax.div(root, 2) == row).astype(jnp.float32)
-        under = (lax.div(root, 2) <= row).astype(jnp.float32)
-        at_home = (lax.rem(root, 2) == col).astype(jnp.float32)
-        return here + 2.0 * under + 4.0 * at_home
-
-    code_mate = jnp.where(low == 0, code_of(owners[0, 1]), code_of(owners[0, 0]))
-    code_own = jnp.where(low == 0, code_of(owners[0, 0]), code_of(owners[0, 1]))
-    note[...] = jnp.full(note.shape, code_mate, jnp.float32)
-
-    @pl.when(hub)
-    def _():
-        told[...] = jnp.full(told.shape, code_own, jnp.float32)
-
-    send_note = remote(note, told, note_send, note_sem, mate)
 
     bar = pltpu.get_barrier_semaphore()
     for target in (
@@ -194,6 +179,29 @@
            for r in (row_up, row_down) for c in range(2) for j in range(n_vec)]
     ):
         pl.semaphore_signal(bar, inc=1, device_id=target, device_id_type=MESH)
+    for w in range(per_dev):
+        load(w).start()
+
+    @pl.when(hub)
+    def _():
+        each(0, pieces, lambda k: own_to_home(k).start())
+
+    def code_of(root):
+        here = (lax.div(root, 2) == row).astype(jnp.float32)
+        under = (lax.div(root, 2) <= row).astype(jnp.float32)
+        at_home = (lax.rem(root, 2) == col).astype(jnp.float32)
+        return here + 2.0 * under + 4.0 * at_home
+
+    code_mate = jnp.where(low == 0, code_of(owners[0, 1]), code_of(owners[0, 0]))
+    code_own = jnp.where(low == 0, code_of(owners[0, 0]), code_of(owners[0, 1]))
+    note[...] = jnp.full(note.shape, code_mate, jnp.float32)
+
+    @pl.when(hub)
+    def _():
+        told[...] = jnp.full(told.shape, code_own, jnp.float32)
+
+    send_note = remote(note, told, note_send, note_sem, mate)
+
     pl.semaphore_wait(bar, 6 * n_vec - 1)
 
     each(0, direct_sent(0), lambda u: direct_unit(u).start())
@@ -251,11 +259,16 @@
                 def _():
                     own_to_mate(i + AHEAD).start()
 
-                own_to_home(i).wait()
+                @pl.when(lax.rem(i, BATCH) == 0)
+                def _():
+                    pltpu.make_async_copy(home_batch(i), home_batch(i), home_sem.at[lax.div(i, BATCH)]).wait()
 
             @pl.when(leaf)
             def _():
-                own_to_mate(i).wait_recv()
+                @pl.when(lax.rem(i, BATCH) == 0)
+                def _():
+                    remote(home_batch(i), home_batch(i), mate_send, home_sem.at[lax.div(i, BATCH)], mate).wait_recv()
+
                 away_to_mate(i).wait_recv()
 
         ku = i - SKEW * row
@@ -304,18 +317,17 @@
     load_at = X_HUB[-1] + Y_LAG + LOAD_LAG
 
     def arrive(n):
-        group(partner, n, vec, x_send, x_sem, across).wait_recv()
-        group(partner, n, vec, y_send, y_sem, over).start()
+        group(partner, n, vec, x_send, x_sem.at[n], across).wait_recv()
+        group(partner, n, vec, y_send, y_sem.at[n], over).start()
         group(partner, n, vec, d_send, d_sem, mate).start()
 
     def pass_on(n):
-        group(partner, n, far_vec, y_send, y_sem, over).wait_recv()
+        group(partner, n, far_vec, y_send, y_sem.at[n], over).wait_recv()
         group(partner, n, far_vec, r_send, r_sem, mate).start()
 
     def load_partner():
-        for n in range(len(groups)):
-            group(partner, n, vec, d_send, d_sem, mate).wait_recv()
-            group(partner, n, vec, r_send, r_sem, mate).wait_recv()
+        quarter_of(partner, d_send, d_sem).wait_recv()
+        quarter_of(partner, r_send, r_sem).wait_recv()
         for w in range(per_dev):
             load(per_dev + w).start()
 
@@ -324,12 +336,12 @@
             load(first + w).wait()
 
     def z_arrive(n):
-        group(beyond, n, vec, zy_send, z_sem, z_to).wait_recv()
-        group(beyond, n, vec, zy_send, zy_sem, over).start()
+        group(beyond, n, vec, zy_send, z_sem.at[n], z_to).wait_recv()
+        group(beyond, n, vec, zy_send, zy_sem.at[n], over).start()
         group(beyond, n, vec, zd_send, zd_sem, mate).start()
 
     def z_pass_on(n):
-        group(beyond, n, far_vec, zy_send, zy_sem, over).wait_recv()
+        group(beyond, n, far_vec, zy_send, zy_sem.at[n], over).wait_recv()
         group(beyond, n, far_vec, zr_send, zr_sem, mate).start()
 
     half = DEEP // 2
@@ -391,11 +403,14 @@
 
     def tell(n):
         target, where = readers[n]
-        return remote(result, table.at[where], t_send.at[n], t_sem.at[where], target)
+        return remote(result, table.at[where], t_send, t_sem, target)
+
+    keep = pltpu.make_async_copy(result, table.at[place], keep_sem)
 
     def tell_all():
         for n in range(len(readers)):
             tell(n).start()
+        keep.start()
 
     events, rest = [], []
     for times, z_times, role in ((X_HUB, Z_HUB, hub), (X_LEAF, Z_LEAF, leaf)):
@@ -460,14 +475,12 @@
     for run in after:
         run()
 
-    table[place] = result[...]
-
-    for n in range(len(groups)):
-        group(beyond, n, vec, zd_send, zd_sem, mate).wait_recv()
-        group(beyond, n, vec, zr_send, zr_sem, mate).wait_recv()
+
+    quarter_of(beyond, zd_send, zd_sem).wait_recv()
+    quarter_of(beyond, zr_send, zr_sem).wait_recv()
 
     def all_sent(buffer, send, target):
-        remote(buffer, buffer, send, t_sem.at[0], target).wait_send()
+        remote(buffer, buffer, send, t_sem, target).wait_send()
 
     @pl.when(hub)
     def _():
@@ -494,20 +507,20 @@
     ):
         all_sent(part, send, target)
 
-    each(skip, units, lambda u: z_unit(u).wait_send())
+    keep.wait()
+    for count in range(min(DIRECT[0], DIRECT_WRAP), max(DIRECT[2], DIRECT_WRAP) + 1):
+        @pl.when(skip == count)
+        def _():
+            some = partner.at[:, pl.ds(0, (units - count) * UNIT)]
+            all_sent(some, z_send, z_to)
+
     each(0, direct_count(order_own), lambda u: direct_unit(u).wait_send())
     each(0, direct_count(lax.rem(order_own + last, rows)), lambda u: relay_unit(u).wait_send())
 
-    for n in range(len(readers)):
-        tell(n).wait_send()
-
-    for j in range(1, n_vec):
-        v = lax.rem(vec + j, n_vec)
-        remote(result, table.at[0], t_send.at[0], t_sem.at[col * n_vec + v], mate).wait_recv()
-    for j in range(n_vec):
-        remote(result, table.at[0], t_send.at[0], t_sem.at[(1 - col) * n_vec + j], mate).wait_recv()
-    for j in range(2 * n_vec):
-        remote(result, table.at[0], t_send.at[0], t_sem.at[2 * n_vec + j], mate).wait_recv()
+    heard = table.at[pl.ds(0, len(readers))]
+    remote(heard, heard, t_send, t_sem, mate).wait_send()
+
+    remote(heard, heard, t_send, t_sem, mate).wait_recv()
 
 
 def step_all(n_walk, n_vec, owners, chol, walkers):
@@ -516,6 +529,7 @@
     pieces = orbitals // LANES
     units = height // n_vec // UNIT
     groups = -(-units // GROUP)
+    most = max(DIRECT[2], DIRECT_WRAP)
     big = pltpu.VMEM((pieces, electrons, LANES), chol.dtype)
     dma = pltpu.SemaphoreType.DMA
     any_spec = pl.BlockSpec(memory_space=pl.ANY)
@@ -525,7 +539,7 @@
         functools.partial(step_kernel, n_walk, n_vec),
         out_shape=(jax.ShapeDtypeStruct((4 * n_vec, 8, 128), jnp.float32), same, same),
         in_specs=[smem, any_spec, any_spec],
-        out_specs=(pl.BlockSpec(memory_space=pltpu.VMEM), any_spec, any_spec),
+        out_specs=(any_spec, any_spec, any_spec),
         scratch_shapes=[
             big, big, big, big, big,
             pltpu.VMEM((max(DIRECT[2], DIRECT_WRAP), per_dev, UNIT, width), walkers.dtype),
@@ -534,8 +548,8 @@
             pltpu.VMEM((8, 128), jnp.float32),
             pltpu.VMEM((8, 128), jnp.float32),
             pltpu.VMEM((8, 128), jnp.float32),
-        ] + [dma((pieces,))] * 4 + [dma] * 12 + [dma((units,))] * 4 + [dma((groups,))] * 8
-        + [dma((2 * per_dev,)), dma, dma, dma((4 * n_vec - 1,)), dma((4 * n_vec,))],
+        ] + [dma((-(-pieces // BATCH),))] + [dma((pieces,))] * 3 + [dma] * 12 + [dma] + [dma((most,))] * 3 + [dma((groups,))] * 4 + [dma] * 4
+        + [dma((2 * per_dev,)), dma, dma, dma, dma, dma],
         compiler_params=pltpu.CompilerParams(
             collective_id=0, has_side_effects=True, vmem_limit_bytes=62 * 1024 * 1024),
         name="step_all",

time: 153 us -> 151 us (0.987)
  Pallas kernels: 152 us -> 150 us
    pallas_call x1, Pallas kernels: 145 us -> 143 us  [step_all(): pl.pallas_call(functools.partial(step_kernel, n_walk, n_vec), out_shape=(...]
where the time goes in v3:
time: 151 us
  Pallas kernels  150 us (99%)
    pallas_call x1, Pallas kernels, step_all(): pl.pallas_call(functools.partial(step_kernel, n_walk, n_vec), out_shape=(...  143 us
    pallas_call x1, Pallas kernels, branch(): pl.pallas_call(functools.partial(branch_kernel, n_walk, n_vec), out_shape...  7.45 us

profile of v3, /device:TPU:0, one launch (start us, length us, event | category | flops | bytes accessed | tf_op | source)
XLA Modules:
  0.0 150.7 jit_solution(15085825797738087991)
XLA Ops:
  0.6 142.6 %step_all.1 = (f32[16,8,128]{2,1,0:T(8,128)}, bf16[2,2432,768]{2,1,0:T(8,128)(2,1)}, bf16[2,2432,768]{2,1,0:T(8,128)(2,1)}) custom-call(s32[1,2]{1,0:T(1,128)} %owners.1, bf16[1,1,384,4096]{3,2,1,0:T(8,128)(2,1)} %chol.1, bf16[2,2432,768]{2,1,0:T(8,128)(2,1)} %walkers.3), custom_call_target="tpu_custom_call" | custom-call | tf_op jit(solution)/shard_map/step_all/pallas_call | solution.py:538
  143.2 7.5 %branch.1 = (bf16[2,2432,768]{2,1,0:T(8,128)(2,1)}, f32[2,2,2]{2,1,0:T(2,128)}, f32[2,2]{1,0:T(2,128)}) custom-call(s32[2]{0:T(128)} %slots.1, bf16[2,2432,768]{2,1,0:T(8,128)(2,1)} %walkers.3, bf16[2,2432,768]{2,1,0:T(8,128)(2,1)} %get-tuple-element.6.partner, bf16[2,2432,768]{2,1,0:T(8,128)(2,1)} %get-tuple-element.7.beyond, ...), custom_call_target="tpu_custom_call" | custom-call | tf_op jit(solution)/shard_map/branch/pallas_call | solution.py:622

commit v4 on v3

--- a/solution.py
+++ b/solution.py
@@ -15,16 +15,17 @@
 SKEW = 3
 AHEAD = 8
 BATCH = 4
-X_SLOW = (16, 100)
+X_SLOW = (17, 100)
 X_FAST = 2
 X_HUB = (16, 17, 18, 19, 20, 21, 23, 24, 25, 25)
-X_LEAF = (3, 5, 7, 8, 10, 11, 12, 14, 15, 16)
+X_LEAF = (6, 7, 9, 10, 12, 13, 14, 16, 17, 18)
 Y_LAG = 3
 LOAD_LAG = 2
-CATCH_UP = 2
+CATCH_UP = 1
 Z_HUB = (16, 33)
-Z_LEAF = (5, 32)
-Z_LAG = 3
+Z_LEAF = (8, 34)
+HUB_START = 3
+Z_LAG = 4
 Z_LAG_Y = 3
 NEAR = 41
 RELAY = 22
@@ -210,7 +211,6 @@
     def _():
         send_note.start()
         each(0, min(AHEAD, pieces), lambda k: own_to_mate(k).start())
-        each(0, units, lambda u: x_unit(u).start())
 
     @pl.when(leaf)
     def _():
@@ -412,7 +412,11 @@
             tell(n).start()
         keep.start()
 
+    def hub_units():
+        each(0, units, lambda u: x_unit(u).start())
+
     events, rest = [], []
+    events.append((HUB_START, hub, functools.partial(hub_units)))
     for times, z_times, role in ((X_HUB, Z_HUB, hub), (X_LEAF, Z_LEAF, leaf)):
         late = []
         for n, end in enumerate(ends):

time: 151 us -> 150 us (level)
  no operation moved by 1% of the time
where the time goes in v4:
time: 150 us
  Pallas kernels  149 us (99%)
    pallas_call x1, Pallas kernels, step_all(): pl.pallas_call(functools.partial(step_kernel, n_walk, n_vec), out_shape=(...  142 us
    pallas_call x1, Pallas kernels, branch(): pl.pallas_call(functools.partial(branch_kernel, n_walk, n_vec), out_shape...  7.45 us

profile of v4, /device:TPU:0, one launch (start us, length us, event | category | flops | bytes accessed | tf_op | source)
XLA Modules:
  0.0 150.1 jit_solution(15430603121321326278)
XLA Ops:
  0.6 142.0 %step_all.1 = (f32[16,8,128]{2,1,0:T(8,128)}, bf16[2,2432,768]{2,1,0:T(8,128)(2,1)}, bf16[2,2432,768]{2,1,0:T(8,128)(2,1)}) custom-call(s32[1,2]{1,0:T(1,128)} %owners.1, bf16[1,1,384,4096]{3,2,1,0:T(8,128)(2,1)} %chol.1, bf16[2,2432,768]{2,1,0:T(8,128)(2,1)} %walkers.3), custom_call_target="tpu_custom_call" | custom-call | tf_op jit(solution)/shard_map/step_all/pallas_call | solution.py:542
  142.6 7.5 %branch.1 = (bf16[2,2432,768]{2,1,0:T(8,128)(2,1)}, f32[2,2,2]{2,1,0:T(2,128)}, f32[2,2]{1,0:T(2,128)}) custom-call(s32[2]{0:T(128)} %slots.1, bf16[2,2432,768]{2,1,0:T(8,128)(2,1)} %walkers.3, bf16[2,2432,768]{2,1,0:T(8,128)(2,1)} %get-tuple-element.6.partner, bf16[2,2432,768]{2,1,0:T(8,128)(2,1)} %get-tuple-element.7.beyond, ...), custom_call_target="tpu_custom_call" | custom-call | tf_op jit(solution)/shard_map/branch/pallas_call | solution.py:626

commit v5 on v4

--- a/solution.py
+++ b/solution.py
@@ -18,13 +18,13 @@
 X_SLOW = (17, 100)
 X_FAST = 2
 X_HUB = (16, 17, 18, 19, 20, 21, 23, 24, 25, 25)
-X_LEAF = (6, 7, 9, 10, 12, 13, 14, 16, 17, 18)
+X_LEAF = (4, 6, 8, 9, 11, 12, 13, 15, 16, 17)
 Y_LAG = 3
 LOAD_LAG = 2
 CATCH_UP = 1
 Z_HUB = (16, 33)
-Z_LEAF = (8, 34)
-HUB_START = 3
+Z_LEAF = (6, 33)
+HUB_START = 0
 Z_LAG = 4
 Z_LAG_Y = 3
 NEAR = 41

time: 150 us -> 149 us (level)
  no operation moved by 1% of the time
where the time goes in v5:
time: 149 us
  Pallas kernels  148 us (99%)
    pallas_call x1, Pallas kernels, step_all(): pl.pallas_call(functools.partial(step_kernel, n_walk, n_vec), out_shape=(...  141 us
    pallas_call x1, Pallas kernels, branch(): pl.pallas_call(functools.partial(branch_kernel, n_walk, n_vec), out_shape...  7.45 us

profile of v5, /device:TPU:0, one launch (start us, length us, event | category | flops | bytes accessed | tf_op | source)
XLA Modules:
  0.0 148.8 jit_solution(9067888293155910665)
XLA Ops:
  0.6 140.8 %step_all.1 = (f32[16,8,128]{2,1,0:T(8,128)}, bf16[2,2432,768]{2,1,0:T(8,128)(2,1)}, bf16[2,2432,768]{2,1,0:T(8,128)(2,1)}) custom-call(s32[1,2]{1,0:T(1,128)} %owners.1, bf16[1,1,384,4096]{3,2,1,0:T(8,128)(2,1)} %chol.1, bf16[2,2432,768]{2,1,0:T(8,128)(2,1)} %walkers.3), custom_call_target="tpu_custom_call" | custom-call | tf_op jit(solution)/shard_map/step_all/pallas_call | solution.py:542
  141.4 7.5 %branch.1 = (bf16[2,2432,768]{2,1,0:T(8,128)(2,1)}, f32[2,2,2]{2,1,0:T(2,128)}, f32[2,2]{1,0:T(2,128)}) custom-call(s32[2]{0:T(128)} %slots.1, bf16[2,2432,768]{2,1,0:T(8,128)(2,1)} %walkers.3, bf16[2,2432,768]{2,1,0:T(8,128)(2,1)} %get-tuple-element.6.partner, bf16[2,2432,768]{2,1,0:T(8,128)(2,1)} %get-tuple-element.7.beyond, ...), custom_call_target="tpu_custom_call" | custom-call | tf_op jit(solution)/shard_map/branch/pallas_call | solution.py:626

commit v6 on v5

--- a/solution.py
+++ b/solution.py
@@ -15,6 +15,7 @@
 SKEW = 3
 AHEAD = 8
 BATCH = 4
+RING = 16
 X_SLOW = (17, 100)
 X_FAST = 2
 X_HUB = (16, 17, 18, 19, 20, 21, 23, 24, 25, 25)
@@ -122,10 +123,10 @@
         return remote(away.at[k], away.at[k], relay_send, away_sem.at[k], mate)
 
     def send_up(k):
-        return remote(up.at[k], up.at[k], up_send, up_sem.at[k], above)
+        return remote(up.at[k], up.at[k], up_send, up_sem.at[lax.rem(k, up_sem.shape[0])], above)
 
     def send_down(k):
-        return remote(down.at[k], down.at[k], down_send, down_sem.at[k], below)
+        return remote(down.at[k], down.at[k], down_send, down_sem.at[lax.rem(k, down_sem.shape[0])], below)
 
     def unit_rows(u):
         return pl.ds(pl.multiple_of(vec * quarter + u * UNIT, UNIT), UNIT)
@@ -389,14 +390,31 @@
         v = jnp.dot(m[:, electrons:], o, preferred_element_type=jnp.float32)
         g_re = u[:, :electrons] - v[:, electrons:]
         g_im = u[:, electrons:] + v[:, :electrons]
-        t_re, t_im = g_re.T, g_im.T
-        eye = (lax.broadcasted_iota(jnp.int32, g_re.shape, 0)
-               == lax.broadcasted_iota(jnp.int32, g_re.shape, 1))
+        side = LANES if electrons % LANES == 0 else electrons
+        eye = (lax.broadcasted_iota(jnp.int32, (side, side), 0)
+               == lax.broadcasted_iota(jnp.int32, (side, side), 1))
+        spots = range(0, electrons, side)
+
+        def tile(g, a, b):
+            return g[a:a + side, b:b + side]
+
+        ex_re = ex_im = bias_re = bias_im = jnp.zeros((side, side), jnp.float32)
+        for a in spots:
+            bias_re = bias_re + tile(g_re, a, a)
+            bias_im = bias_im + tile(g_im, a, a)
+            for b in spots:
+                if b < a:
+                    continue
+                times = 1.0 if a == b else 2.0
+                re, im = tile(g_re, a, b), tile(g_im, a, b)
+                t_re, t_im = tile(g_re, b, a).T, tile(g_im, b, a).T
+                ex_re = ex_re + times * (re * t_re - im * t_im)
+                ex_im = ex_im + times * (re * t_im + im * t_re)
         values = [
-            jnp.sum(jnp.where(eye, g_re, 0.0)),
-            jnp.sum(jnp.where(eye, g_im, 0.0)),
-            jnp.sum(g_re * t_re - g_im * t_im),
-            2.0 * jnp.sum(g_re * t_im),
+            jnp.sum(jnp.where(eye, bias_re, 0.0)),
+            jnp.sum(jnp.where(eye, bias_im, 0.0)),
+            jnp.sum(ex_re),
+            jnp.sum(ex_im),
         ]
         for n, value in enumerate(values):
             result[...] = jnp.where(jnp.logical_and(sub == w, lane == n), value, result[...])
@@ -534,6 +552,7 @@
     units = height // n_vec // UNIT
     groups = -(-units // GROUP)
     most = max(DIRECT[2], DIRECT_WRAP)
+    ring = RING if SKEW * (n_walk // 2 - 1) < RING < pieces else pieces
     big = pltpu.VMEM((pieces, electrons, LANES), chol.dtype)
     dma = pltpu.SemaphoreType.DMA
     any_spec = pl.BlockSpec(memory_space=pl.ANY)
@@ -552,7 +571,7 @@
             pltpu.VMEM((8, 128), jnp.float32),
             pltpu.VMEM((8, 128), jnp.float32),
             pltpu.VMEM((8, 128), jnp.float32),
-        ] + [dma((-(-pieces // BATCH),))] + [dma((pieces,))] * 3 + [dma] * 12 + [dma] + [dma((most,))] * 3 + [dma((groups,))] * 4 + [dma] * 4
+        ] + [dma((-(-pieces // BATCH),))] + [dma((pieces,))] + [dma((ring,))] * 2 + [dma] * 12 + [dma] + [dma((most,))] * 3 + [dma((groups,))] * 4 + [dma] * 4
         + [dma((2 * per_dev,)), dma, dma, dma, dma, dma],
         compiler_params=pltpu.CompilerParams(
             collective_id=0, has_side_effects=True, vmem_limit_bytes=62 * 1024 * 1024),

time: 149 us -> 149 us (level)
  no operation moved by 1% of the time
where the time goes in v6:
time: 149 us
  Pallas kernels  148 us (99%)
    pallas_call x1, Pallas kernels, step_all(): pl.pallas_call(functools.partial(step_kernel, n_walk, n_vec), out_shape=(...  140 us
    pallas_call x1, Pallas kernels, branch(): pl.pallas_call(functools.partial(branch_kernel, n_walk, n_vec), out_shape...  7.55 us

profile of v6, /device:TPU:0, one launch (start us, length us, event | category | flops | bytes accessed | tf_op | source)
XLA Modules:
  0.0 148.6 jit_solution(4530831192475999271)
XLA Ops:
  0.6 140.4 %step_all.1 = (f32[16,8,128]{2,1,0:T(8,128)}, bf16[2,2432,768]{2,1,0:T(8,128)(2,1)}, bf16[2,2432,768]{2,1,0:T(8,128)(2,1)}) custom-call(s32[1,2]{1,0:T(1,128)} %owners.1, bf16[1,1,384,4096]{3,2,1,0:T(8,128)(2,1)} %chol.1, bf16[2,2432,768]{2,1,0:T(8,128)(2,1)} %walkers.3), custom_call_target="tpu_custom_call" | custom-call | tf_op jit(solution)/shard_map/step_all/pallas_call | solution.py:561
  141.1 7.5 %branch.1 = (bf16[2,2432,768]{2,1,0:T(8,128)(2,1)}, f32[2,2,2]{2,1,0:T(2,128)}, f32[2,2]{1,0:T(2,128)}) custom-call(s32[2]{0:T(128)} %slots.1, bf16[2,2432,768]{2,1,0:T(8,128)(2,1)} %walkers.3, bf16[2,2432,768]{2,1,0:T(8,128)(2,1)} %get-tuple-element.6.partner, bf16[2,2432,768]{2,1,0:T(8,128)(2,1)} %get-tuple-element.7.beyond, ...), custom_call_target="tpu_custom_call" | custom-call | tf_op jit(solution)/shard_map/branch/pallas_call | solution.py:645

commit v7 on v6

--- a/solution.py
+++ b/solution.py
@@ -16,16 +16,16 @@
 AHEAD = 8
 BATCH = 4
 RING = 16
-X_SLOW = (17, 100)
+X_SLOW = (16, 100)
 X_FAST = 2
 X_HUB = (16, 17, 18, 19, 20, 21, 23, 24, 25, 25)
-X_LEAF = (4, 6, 8, 9, 11, 12, 13, 15, 16, 17)
+X_LEAF = (6, 7, 9, 10, 12, 13, 14, 16, 17, 18)
 Y_LAG = 3
 LOAD_LAG = 2
 CATCH_UP = 1
 Z_HUB = (16, 33)
-Z_LEAF = (6, 33)
-HUB_START = 0
+Z_LEAF = (8, 34)
+HUB_START = 3
 Z_LAG = 4
 Z_LAG_Y = 3
 NEAR = 41

time: 149 us -> 148 us (level)
  no operation moved by 1% of the time
where the time goes in v7:
time: 148 us
  Pallas kernels  148 us (100%)
    pallas_call x1, Pallas kernels, step_all(): pl.pallas_call(functools.partial(step_kernel, n_walk, n_vec), out_shape=(...  140 us
    pallas_call x1, Pallas kernels, branch(): pl.pallas_call(functools.partial(branch_kernel, n_walk, n_vec), out_shape...  7.45 us

profile of v7, /device:TPU:0, one launch (start us, length us, event | category | flops | bytes accessed | tf_op | source)
XLA Modules:
  0.0 148.2 jit_solution(13596046381617024176)
XLA Ops:
  0.6 140.2 %step_all.1 = (f32[16,8,128]{2,1,0:T(8,128)}, bf16[2,2432,768]{2,1,0:T(8,128)(2,1)}, bf16[2,2432,768]{2,1,0:T(8,128)(2,1)}) custom-call(s32[1,2]{1,0:T(1,128)} %owners.1, bf16[1,1,384,4096]{3,2,1,0:T(8,128)(2,1)} %chol.1, bf16[2,2432,768]{2,1,0:T(8,128)(2,1)} %walkers.3), custom_call_target="tpu_custom_call" | custom-call | tf_op jit(solution)/shard_map/step_all/pallas_call | solution.py:561
  140.8 7.5 %branch.1 = (bf16[2,2432,768]{2,1,0:T(8,128)(2,1)}, f32[2,2,2]{2,1,0:T(2,128)}, f32[2,2]{1,0:T(2,128)}) custom-call(s32[2]{0:T(128)} %slots.1, bf16[2,2432,768]{2,1,0:T(8,128)(2,1)} %walkers.3, bf16[2,2432,768]{2,1,0:T(8,128)(2,1)} %get-tuple-element.6.partner, bf16[2,2432,768]{2,1,0:T(8,128)(2,1)} %get-tuple-element.7.beyond, ...), custom_call_target="tpu_custom_call" | custom-call | tf_op jit(solution)/shard_map/branch/pallas_call | solution.py:645
